TPU v7x, 32 devices: a whole 2x2x4 slice. The times are simulated.
32 devices in a mesh: group: 4 (over y, x), member: 8 (over z, core).
Axes of the slice: x: 2, y: 2, z: 4, core: 2. Of those that a mesh axis runs over, the one named last changes fastest.
Arguments:
- activations: bfloat16 [4, 1024, 2048], P('group', 'member'), may hold values from -6 to 6
- lengths: int32 [4, 8], P('group'), may hold values from 1 to 128, 576 in all within a row
- assignment: int32 [4, 8], P('group'), may hold values from 0 to 7, each once within a row
- owners: int32 [4], replicated, may hold values from 0 to 3
- prefix_cache: bfloat16 [4, 8192, 256], P('group', 'member'), may hold values from -244 to 244
- first_gain: float32 [2048], replicated, may hold values from 0.1 to 1.9
- first_bias: float32 [2048], replicated, may hold values from -3 to 3
- query_weight: bfloat16 [2048, 2048], replicated, may hold values from -0.125 to 0.125
- keyval_weight: bfloat16 [2048, 256], replicated, may hold values from -0.4375 to 0.4375
- output_weight: bfloat16 [2048, 2048], replicated, may hold values from -0.125 to 0.125
- second_gain: float32 [2048], replicated, may hold values from 0.1 to 1.9
- second_bias: float32 [2048], replicated, may hold values from -3 to 3
- expand_weight: bfloat16 [2048, 8192], P(None, 'member'), may hold values from -0.125 to 0.125
- contract_weight: bfloat16 [8192, 2048], P('member'), may hold values from -0.0625 to 0.0625
Outputs:
- layer_output: bfloat16 [4, 1024, 2048], P('group', 'member')
Inputs may be any that keep to these rules, and one draw needn't show every extreme that they name: Each row of lengths sums to 576 and its longest entry is 128. Each row of assignment names every request of its group once. `owners`: several groups may attend the same cache slot.
All inputs are finite; a program needn't handle non-finite values.
Results may differ from a plain program's by a relative error of at most 0.011.
The roundings to bfloat16 on the way count: a program that leaves them out, or rounds other values in their place, can miss the bound.
Values may be sent and summed in bfloat16 or wider, within the bound.
No kernel may reach another device: no remote copies, remote signals or barrier semaphores. Data moves between devices by JAX's collectives and lax.ppermute only.
A program may use at most 128 MiB of HBM per device.

v0:
```python
import math

import jax
import jax.numpy as jnp
from jax import lax
from jax.sharding import PartitionSpec as P

EPSILON = 1e-05
NEGATIVE = -1e30


def layer_norm(values, gain, bias):
    average = jnp.mean(values, axis=-1, keepdims=True)
    centered = values - average
    spread = jnp.mean(centered * centered, axis=-1, keepdims=True)
    return centered * lax.rsqrt(spread + EPSILON) * gain + bias


def pick_value(table, wanted):
    slots_at = lax.broadcasted_iota(jnp.int32, table.shape, 0)
    return jnp.sum(jnp.where(slots_at == wanted, table, 0))


def own_scores(query_block, own_keys, scaling):
    scores = (
        jnp.einsum("thd,sd->ths", query_block, own_keys, preferred_element_type=jnp.float32)
        * scaling
    )
    block_rows = query_block.shape[0]
    key_rows = own_keys.shape[0]
    row_at = lax.broadcasted_iota(jnp.int32, (block_rows, 1, key_rows), 0)
    column_at = lax.broadcasted_iota(jnp.int32, (block_rows, 1, key_rows), 2)
    return jnp.where(column_at <= row_at, scores, NEGATIVE)


def folded_attention(queries, keys_values, selected):
    row_count, head_count, head_size = queries.shape
    scaling = 1.0 / math.sqrt(head_size)
    own_keys = keys_values[:, :head_size]
    own_values = keys_values[:, head_size:]
    suffix_scores = own_scores(queries, own_keys, scaling)
    highest = jnp.max(suffix_scores, axis=-1)
    suffix_exp = jnp.exp(suffix_scores - highest[..., None])
    denominator = jnp.sum(suffix_exp, axis=-1)
    weighted = jnp.einsum(
        "ths,sd->thd",
        suffix_exp.astype(jnp.bfloat16),
        own_values,
        preferred_element_type=jnp.float32,
    )
    running = (weighted, highest, denominator)
    portion = lax.all_gather(selected, "member", axis=0, tiled=True)
    extent = portion.shape[0]
    stride = math.gcd(extent, 1024)

    def advance(state_now, block_index):
        weighted_now, highest_now, denominator_now = state_now
        key_block = lax.dynamic_slice_in_dim(portion, block_index * stride, stride, 0)
        scores = (
            jnp.einsum(
                "thd,pd->thp", queries, key_block[:, :head_size], preferred_element_type=jnp.float32
            )
            * scaling
        )
        highest_next = jnp.maximum(highest_now, jnp.max(scores, axis=-1))
        rescale = jnp.exp(highest_now - highest_next)
        exponent = jnp.exp(scores - highest_next[..., None])
        denominator_next = denominator_now * rescale + jnp.sum(exponent, axis=-1)
        weighted_next = weighted_now * rescale[..., None] + jnp.einsum(
            "thp,pd->thd",
            exponent.astype(jnp.bfloat16),
            key_block[:, head_size:],
            preferred_element_type=jnp.float32,
        )
        return ((weighted_next, highest_next, denominator_next), None)

    running, _ = lax.scan(advance, running, jnp.arange(extent // stride, dtype=jnp.int32))
    weighted, highest, denominator = running
    return (
        (weighted / denominator[..., None])
        .astype(jnp.bfloat16)
        .reshape(row_count, head_count * head_size)
    )


def shards(
    activations,
    lengths,
    assignment,
    owners,
    prefix_cache,
    first_gain,
    first_bias,
    query_weight,
    keyval_weight,
    output_weight,
    second_gain,
    second_bias,
    expand_weight,
    contract_weight,
):
    group_index = lax.axis_index("group")
    member_index = lax.axis_index("member")
    request = pick_value(assignment[0], member_index)
    length_here = pick_value(lengths[0], request)
    owner_here = pick_value(owners, group_index)
    tokens = activations[0]
    row_count = tokens.shape[0]
    head_size = prefix_cache.shape[2] // 2
    head_count = tokens.shape[1] // head_size
    every_block = lax.all_gather(prefix_cache, "group", axis=0, tiled=True)
    selected = lax.dynamic_index_in_dim(every_block, owner_here, 0, keepdims=False)
    tokens_wide = tokens.astype(jnp.float32)
    normed = layer_norm(tokens_wide, first_gain, first_bias).astype(jnp.bfloat16)
    queries = jnp.dot(normed, query_weight, preferred_element_type=jnp.float32).astype(jnp.bfloat16)
    queries = queries.reshape(row_count, head_count, head_size)
    keys_values = jnp.dot(normed, keyval_weight, preferred_element_type=jnp.float32).astype(
        jnp.bfloat16
    )
    attended = folded_attention(queries, keys_values, selected)
    residual = tokens_wide + jnp.dot(attended, output_weight, preferred_element_type=jnp.float32)
    second = layer_norm(residual, second_gain, second_bias).astype(jnp.bfloat16)
    hidden = jax.nn.gelu(
        jnp.dot(
            lax.all_gather(second, "member", axis=0, tiled=True),
            expand_weight,
            preferred_element_type=jnp.float32,
        ),
        approximate=True,
    ).astype(jnp.bfloat16)
    summed = lax.psum_scatter(
        jnp.dot(hidden, contract_weight, preferred_element_type=jnp.float32).astype(jnp.bfloat16),
        "member",
        scatter_dimension=0,
        tiled=True,
    ).astype(jnp.float32)
    is_live = lax.broadcasted_iota(jnp.int32, (row_count, 1), 0) < length_here
    return jnp.where(is_live, residual + summed, 0.0).astype(jnp.bfloat16)[None]


def solution(mesh):
    return jax.shard_map(
        shards,
        mesh=mesh,
        in_specs=(
            P("group", "member", None),
            P("group", None),
            P("group", None),
            P(),
            P("group", "member", None),
            P(),
            P(),
            P(),
            P(),
            P(),
            P(),
            P(),
            P(None, "member"),
            P("member", None),
        ),
        out_specs=P("group", "member", None),
        check_vma=False,
    )
```

profile of v0, /device:TPU:0, one launch (start us, length us, event | category | flops | bytes accessed | tf_op | source)
XLA Modules:
  0.0 286.6 jit_solution(2638500522030421383)
XLA Ops:
  10.5 36.7 %all-gather.5.cloned.1.call-done = bf16[4,1024,256]{2,1,0:T(8,128)(2,1)} async-done(((bf16[1,1024,256]{2,1,0:T(8,128)(2,1)}), bf16[4,1024,256]{2,1,0:T(8,128)(2,1)}) %all-gather.5.cloned.1.call-update) | async-done | bytes 2097168 | tf_op jit(solution)/shard_map/all_gather | solution.py:111
  51.8 5.0 %fusion.30 = bf16[16,16,8,128]{3,2,1,0:T(8,128)(2,1)S(1)} fusion(bf16[2048,2048]{1,0:T(8,128)(2,1)} %param.23, bf16[1,128,2048]{2,1,0:T(8,128)(2,1)} %param.16, f32[2048]{0:T(1024)} %param.22, f32[2048]{0:T(1024)} %param.21, f32[128]{0:T(128)S(1)} %add_rsqrt_fusion.1, f32[128]{0:T(128)S(1)} %broadcast_multiply_fusion.1), kind=kOutput, calls=%fused_computation.39 | convolution fusion | flops 1075576832 | bytes 9454592 | tf_op jit(solution)/shard_map/dot_general | solution.py:115
  58.2 38.3 %all-gather.9.cloned.1.call-done = bf16[1,8192,256]{2,1,0:T(8,128)(2,1)} async-done(((bf16[1,1024,256]{2,1,0:T(8,128)(2,1)}), bf16[1,8192,256]{2,1,0:T(8,128)(2,1)}) %all-gather.9.cloned.1.call-update) | async-done | bytes 4194320 | tf_op jit(solution)/shard_map/all_gather | solution.py:52
  96.4 62.7 %while.14 = (s32[]{:T(128)}, f32[128,16,128]{2,0,1:T(8,128)S(1)}, f32[128,16]{0,1:T(8,128)S(1)}, f32[128,16]{0,1:T(8,128)S(1)}, s32[8]{0:T(128)S(1)}, /*index=5*...) while((s32[]{:T(128)}, f32[128,16,128]{2,0,1:T(8,128)S(1)}, ...), condition=%wide.region_10.11_spmd, body=%wide.region_7.10_spmd.sunk | while | flops 1091047424 | bytes 28442832 | solution.py:77
  97.7 2.2 bitcast_reduce_fusion.2
  101.3 2.9 %fusion.69 = f32[128,16,128]{2,0,1:T(8,128)S(1)} fusion(f32[1024,128,16]{1,0,2:T(8,128)S(1)} %get-tuple-element.135, f32[128,16]{0,1:T(8,128)S(1)} %max.4, f32[128,16,128]{2,0,1:T(8,128)S(1)} %get-tuple-element.152, f32[128,16]{0,1:T(8,128)S(1)} %get-tuple-element.137, bf16[8192,256]{1,0:T(8,128)(2,1)} %get-tuple-element.168, s32[]{:T(128)S(6)} %select_n.46, ...), kind=kOutput, calls=%fused_computation.8.clone.1 | convolution fusion | flops 543686656 | bytes 10764296 | tf_op jit(solution)/shard_map/while/body/eval_jaxpr/thp,pd->thd/dot_general | solution.py:69
  105.5 2.2 bitcast_reduce_fusion.2
  109.2 2.9 %fusion.69 = f32[128,16,128]{2,0,1:T(8,128)S(1)} fusion(f32[1024,128,16]{1,0,2:T(8,128)S(1)} %get-tuple-element.135, f32[128,16]{0,1:T(8,128)S(1)} %max.4, f32[128,16,128]{2,0,1:T(8,128)S(1)} %get-tuple-element.152, f32[128,16]{0,1:T(8,128)S(1)} %get-tuple-element.137, bf16[8192,256]{1,0:T(8,128)(2,1)} %get-tuple-element.168, s32[]{:T(128)S(6)} %select_n.46, ...), kind=kOutput, calls=%fused_computation.8.clone.1 | convolution fusion | flops 543686656 | bytes 10764296 | tf_op jit(solution)/shard_map/while/body/eval_jaxpr/thp,pd->thd/dot_general | solution.py:69
  113.4 2.2 bitcast_reduce_fusion.2
  117.0 2.9 %fusion.69 = f32[128,16,128]{2,0,1:T(8,128)S(1)} fusion(f32[1024,128,16]{1,0,2:T(8,128)S(1)} %get-tuple-element.135, f32[128,16]{0,1:T(8,128)S(1)} %max.4, f32[128,16,128]{2,0,1:T(8,128)S(1)} %get-tuple-element.152, f32[128,16]{0,1:T(8,128)S(1)} %get-tuple-element.137, bf16[8192,256]{1,0:T(8,128)(2,1)} %get-tuple-element.168, s32[]{:T(128)S(6)} %select_n.46, ...), kind=kOutput, calls=%fused_computation.8.clone.1 | convolution fusion | flops 543686656 | bytes 10764296 | tf_op jit(solution)/shard_map/while/body/eval_jaxpr/thp,pd->thd/dot_general | solution.py:69
  121.2 2.2 bitcast_reduce_fusion.2
  124.8 2.9 %fusion.69 = f32[128,16,128]{2,0,1:T(8,128)S(1)} fusion(f32[1024,128,16]{1,0,2:T(8,128)S(1)} %get-tuple-element.135, f32[128,16]{0,1:T(8,128)S(1)} %max.4, f32[128,16,128]{2,0,1:T(8,128)S(1)} %get-tuple-element.152, f32[128,16]{0,1:T(8,128)S(1)} %get-tuple-element.137, bf16[8192,256]{1,0:T(8,128)(2,1)} %get-tuple-element.168, s32[]{:T(128)S(6)} %select_n.46, ...), kind=kOutput, calls=%fused_computation.8.clone.1 | convolution fusion | flops 543686656 | bytes 10764296 | tf_op jit(solution)/shard_map/while/body/eval_jaxpr/thp,pd->thd/dot_general | solution.py:69
  129.0 2.2 bitcast_reduce_fusion.2
  132.7 2.9 %fusion.69 = f32[128,16,128]{2,0,1:T(8,128)S(1)} fusion(f32[1024,128,16]{1,0,2:T(8,128)S(1)} %get-tuple-element.135, f32[128,16]{0,1:T(8,128)S(1)} %max.4, f32[128,16,128]{2,0,1:T(8,128)S(1)} %get-tuple-element.152, f32[128,16]{0,1:T(8,128)S(1)} %get-tuple-element.137, bf16[8192,256]{1,0:T(8,128)(2,1)} %get-tuple-element.168, s32[]{:T(128)S(6)} %select_n.46, ...), kind=kOutput, calls=%fused_computation.8.clone.1 | convolution fusion | flops 543686656 | bytes 10764296 | tf_op jit(solution)/shard_map/while/body/eval_jaxpr/thp,pd->thd/dot_general | solution.py:69
  136.9 2.2 bitcast_reduce_fusion.2
  140.5 2.9 %fusion.69 = f32[128,16,128]{2,0,1:T(8,128)S(1)} fusion(f32[1024,128,16]{1,0,2:T(8,128)S(1)} %get-tuple-element.135, f32[128,16]{0,1:T(8,128)S(1)} %max.4, f32[128,16,128]{2,0,1:T(8,128)S(1)} %get-tuple-element.152, f32[128,16]{0,1:T(8,128)S(1)} %get-tuple-element.137, bf16[8192,256]{1,0:T(8,128)(2,1)} %get-tuple-element.168, s32[]{:T(128)S(6)} %select_n.46, ...), kind=kOutput, calls=%fused_computation.8.clone.1 | convolution fusion | flops 543686656 | bytes 10764296 | tf_op jit(solution)/shard_map/while/body/eval_jaxpr/thp,pd->thd/dot_general | solution.py:69
  144.7 2.2 bitcast_reduce_fusion.2
  148.4 2.9 %fusion.69 = f32[128,16,128]{2,0,1:T(8,128)S(1)} fusion(f32[1024,128,16]{1,0,2:T(8,128)S(1)} %get-tuple-element.135, f32[128,16]{0,1:T(8,128)S(1)} %max.4, f32[128,16,128]{2,0,1:T(8,128)S(1)} %get-tuple-element.152, f32[128,16]{0,1:T(8,128)S(1)} %get-tuple-element.137, bf16[8192,256]{1,0:T(8,128)(2,1)} %get-tuple-element.168, s32[]{:T(128)S(6)} %select_n.46, ...), kind=kOutput, calls=%fused_computation.8.clone.1 | convolution fusion | flops 543686656 | bytes 10764296 | tf_op jit(solution)/shard_map/while/body/eval_jaxpr/thp,pd->thd/dot_general | solution.py:69
  152.6 2.2 bitcast_reduce_fusion.2
  156.2 2.9 %fusion.69 = f32[128,16,128]{2,0,1:T(8,128)S(1)} fusion(f32[1024,128,16]{1,0,2:T(8,128)S(1)} %get-tuple-element.135, f32[128,16]{0,1:T(8,128)S(1)} %max.4, f32[128,16,128]{2,0,1:T(8,128)S(1)} %get-tuple-element.152, f32[128,16]{0,1:T(8,128)S(1)} %get-tuple-element.137, bf16[8192,256]{1,0:T(8,128)(2,1)} %get-tuple-element.168, s32[]{:T(128)S(6)} %select_n.46, ...), kind=kOutput, calls=%fused_computation.8.clone.1 | convolution fusion | flops 543686656 | bytes 10764296 | tf_op jit(solution)/shard_map/while/body/eval_jaxpr/thp,pd->thd/dot_general | solution.py:69
  161.9 4.8 %fusion.51 = (f32[128]{0:T(128)S(1)}, f32[128,2048]{1,0:T(8,128)S(1)}) fusion(bf16[128,2048]{0,1:T(8,128)(2,1)S(1)} %bitcast.88, bf16[2048,2048]{1,0:T(8,128)(2,1)} %param.25, bf16[1,128,2048]{2,1,0:T(8,128)(2,1)S(1)} %copy-done.1), kind=kOutput, calls=%fused_computation.76 | convolution fusion | flops 1074528128 | bytes 10486272 | tf_op jit(solution)/shard_map/dot_general | solution.py:121
  168.2 45.8 %all-gather.7.cloned.1.call-done = bf16[1024,2048]{1,0:T(8,128)(2,1)} async-done(((bf16[128,2048]{1,0:T(8,128)(2,1)}), bf16[1024,2048]{1,0:T(8,128)(2,1)}) %all-gather.7.cloned.1.call-update) | async-done | bytes 4194320 | tf_op jit(solution)/shard_map/all_gather | solution.py:125
  214.0 15.1 %convolution_convert_fusion = bf16[1024,2048]{1,0:T(8,128)(2,1)} fusion(bf16[1024,2048]{1,0:T(8,128)(2,1)} %param.29, bf16[1024,2048]{1,0:T(8,128)(2,1)} %all-gather.7.cloned.1.call-done, bf16[2048,1024]{1,0:T(8,128)(2,1)} %param.28), kind=kOutput, calls=%fused_computation.25 | convolution fusion | flops 8601468928 | bytes 16777216 | tf_op jit(solution)/shard_map/dot_general | solution.py:132
  232.2 45.8 %reduce-scatter.2.cloned.1.call-done = bf16[128,2048]{1,0:T(8,128)(2,1)} async-done(((bf16[1024,2048]{1,0:T(8,128)(2,1)}), bf16[128,2048]{1,0:T(8,128)(2,1)}) %reduce-scatter.2.cloned.1.call-update) | async-done | bytes 524304 | tf_op jit(solution)/shard_map/reduce_scatter | solution.py:131
  (87 shorter events, 33.0 us)
Async XLA Ops:
  6.5 50.4 %copy-start = (bf16[2048,256]{1,0:T(8,128)(2,1)S(1)}, bf16[2048,256]{1,0:T(8,128)(2,1)}, u32[]{:S(2)}) copy-start(bf16[2048,256]{1,0:T(8,128)(2,1)} %param.24) | copy-start | bytes 3145732
  6.5 40.7 %all-gather.5.cloned.1.call-start = ((), (), s32[]{:S(2)}) async-start(), calls=%async_computation.1 | async-start | bytes 2621440 | tf_op jit(solution)/shard_map/all_gather | solution.py:111
  7.3 89.2 %all-gather.9.cloned.1.call-start = ((), (), s32[]{:S(2)}) async-start(), calls=%async_computation.4 | async-start | bytes 4718592 | tf_op jit(solution)/shard_map/all_gather | solution.py:52
  49.1 164.9 %all-gather.7.cloned.1.call-start = ((), (), s32[]{:S(2)}) async-start(), calls=%async_computation.2 | async-start | bytes 4718592 | tf_op jit(solution)/shard_map/all_gather | solution.py:125
  51.7 5.2 %copy-start.1 = (bf16[1,128,2048]{2,1,0:T(8,128)(2,1)S(1)}, bf16[1,128,2048]{2,1,0:T(8,128)(2,1)}, u32[]{:S(2)}) copy-start(bf16[1,128,2048]{2,1,0:T(8,128)(2,1)} %param.16) | copy-start | bytes 1572868
  51.7 5.2 %copy-start.4 = (f32[2048]{0:T(1024)S(1)}, f32[2048]{0:T(1024)}, u32[]{:S(2)}) copy-start(f32[2048]{0:T(1024)} %param.22) | copy-start | bytes 24580
  51.8 5.2 %copy-start.5 = (f32[2048]{0:T(1024)S(1)}, f32[2048]{0:T(1024)}, u32[]{:S(2)}) copy-start(f32[2048]{0:T(1024)} %param.21) | copy-start | bytes 24580
  161.8 5.1 %copy-start.2 = (f32[2048]{0:T(1024)S(1)}, f32[2048]{0:T(1024)}, u32[]{:S(2)}) copy-start(f32[2048]{0:T(1024)} %param.27) | copy-start | bytes 24580
  161.9 5.1 %copy-start.3 = (f32[2048]{0:T(1024)S(1)}, f32[2048]{0:T(1024)}, u32[]{:S(2)}) copy-start(f32[2048]{0:T(1024)} %param.26) | copy-start | bytes 24580
  168.0 110.1 %reduce-scatter.2.cloned.1.call-start = ((), (), s32[]{:S(2)}) async-start(), calls=%async_computation.3 | async-start | bytes 4718592 | tf_op jit(solution)/shard_map/reduce_scatter | solution.py:131
  229.1 0.7 copy-start.6
  229.1 1.3 copy-start.7
Sparse Core Ops, SparseCore 0:
  9.2 38.0 all-gather.4
  49.3 47.1 all-gather.8
  168.1 45.8 all-gather.6
  229.3 48.7 reduce-scatter.1
where the time goes:
time: 288 us; the launch traced here: 287 us
  waiting for transfers between devices  167 us (58%)
  matrix products  67.1 us (23%)
  other arithmetic  22.2 us (8%)
  between operations  15.2 us (5%)
  local copies, waits for them, and re-layouts  8.7 us (3%)
  loops' own time  5.68 us (2%)
    reduce_scatter x1, waiting for transfers between devices, shards(): lax.psum_scatter(jnp.dot(hidden, contract_weight, preferred_element_type=...  45.8 us
    all_gather x1, waiting for transfers between devices, shards(): lax.all_gather(second, 'member', axis=0, tiled=True)  45.8 us
    all_gather x1, waiting for transfers between devices, folded_attention(): portion = lax.all_gather(selected, 'member', axis=0, tiled=True)  38.3 us
    all_gather x1, waiting for transfers between devices, shards(): every_block = lax.all_gather(prefix_cache, 'group', axis=0, tiled=True)  36.7 us
    dot_general x8, matrix products, advance(): jnp.einsum('thp,pd->thd', exponent.astype(jnp.bfloat16), key_block[:, hea...  23.5 us
    dot_general x8, matrix products, advance(): jnp.einsum('thd,pd->thp', queries, key_block[:, :head_size], preferred_el...  17.7 us
    dot_general x1, matrix products, shards(): jnp.dot(hidden, contract_weight, preferred_element_type=jnp.float32)  15.1 us
    reduce_sum x8, other arithmetic, advance(): denominator_next = denominator_now * rescale + jnp.sum(exponent, axis=-1)  11 us
  transfers between devices with their start and end apart: 4, of which 4 were waited for; matrix products, arithmetic and copies ran while one was open for 4% of the time, Pallas kernels for 0%

commit v1 on v0

v1 whole, which is shorter than its diff:
```python
import functools
import math

import jax
import jax.numpy as jnp
from jax import lax
from jax.experimental import pallas as pl
from jax.experimental.pallas import tpu as pltpu
from jax.sharding import PartitionSpec as P

EPSILON = 1e-05
NEGATIVE = -1e30
HEADS_AT_ONCE = 2


def layer_norm(values, gain, bias):
    average = jnp.mean(values, axis=-1, keepdims=True)
    centered = values - average
    spread = jnp.mean(centered * centered, axis=-1, keepdims=True)
    return centered * lax.rsqrt(spread + EPSILON) * gain + bias


def pick_value(table, wanted):
    slots_at = lax.broadcasted_iota(jnp.int32, table.shape, 0)
    return jnp.sum(jnp.where(slots_at == wanted, table, 0))


def ring_order(chips):
    return list(range(0, 1)) + list(range(1, chips, 2)) + list(range(chips - 2 + chips % 2, 0, -2))


def attend_kernel(first, last, head_size, *refs):
    refs = list(refs)
    query_ref = refs.pop(0)
    if first:
        own_ref = refs.pop(0)
    else:
        weighted_in, highest_in, denominator_in = refs[:3]
        del refs[:3]
    outs = 1 if last else 3
    block_refs, out_refs = refs[:-outs], refs[-outs:]
    rows = query_ref.shape[0]
    factor = math.log2(math.e) / math.sqrt(head_size)
    queries = jnp.concatenate(
        [query_ref[:, h * head_size : (h + 1) * head_size] for h in range(HEADS_AT_ONCE)], axis=0
    )

    def raw_scores(keys):
        return lax.dot_general(
            queries, keys, (((1,), (1,)), ((), ())), preferred_element_type=jnp.float32
        )

    def apply(scores, values, highest):
        exponent = jnp.exp2((scores - highest) * factor)
        total = jnp.sum(exponent, axis=-1, keepdims=True)
        product = jnp.dot(exponent.astype(jnp.bfloat16), values, preferred_element_type=jnp.float32)
        return product, total

    if first:
        scores = raw_scores(own_ref[:, :head_size])
        row_at = lax.broadcasted_iota(jnp.int32, scores.shape, 0) % rows
        column_at = lax.broadcasted_iota(jnp.int32, scores.shape, 1)
        scores = jnp.where(column_at <= row_at, scores, NEGATIVE)
        highest = jnp.max(scores, axis=-1, keepdims=True)
        weighted, denominator = apply(scores, own_ref[:, head_size:], highest)
    else:
        weighted = jnp.concatenate(
            [weighted_in[:, h * head_size : (h + 1) * head_size] for h in range(HEADS_AT_ONCE)], axis=0
        )
        highest = jnp.concatenate([highest_in[h] for h in range(HEADS_AT_ONCE)], axis=0)
        denominator = jnp.concatenate([denominator_in[h] for h in range(HEADS_AT_ONCE)], axis=0)
    for block_ref in block_refs:
        extent = block_ref.shape[0]
        stride = math.gcd(extent, 1024)
        for start in range(0, extent, stride):
            scores = raw_scores(block_ref[start : start + stride, :head_size])
            highest_next = jnp.maximum(highest, jnp.max(scores, axis=-1, keepdims=True))
            rescale = jnp.exp2((highest - highest_next) * factor)
            product, total = apply(scores, block_ref[start : start + stride, head_size:], highest_next)
            weighted = weighted * rescale + product
            denominator = denominator * rescale + total
            highest = highest_next
    if last:
        weighted = weighted / denominator
    for h in range(HEADS_AT_ONCE):
        part = weighted[h * rows : (h + 1) * rows]
        out_refs[0][:, h * head_size : (h + 1) * head_size] = part.astype(out_refs[0].dtype)
        if not last:
            out_refs[1][h] = highest[h * rows : (h + 1) * rows]
            out_refs[2][h] = denominator[h * rows : (h + 1) * rows]


def attend(queries, own, state, blocks, last, head_size):
    rows, width = queries.shape
    heads = width // head_size
    wide = HEADS_AT_ONCE * head_size
    first = state is None
    flat = pl.BlockSpec((rows, wide), lambda i: (0, i))
    stat = pl.BlockSpec((HEADS_AT_ONCE, rows, 1), lambda i: (i, 0, 0))
    whole = lambda array: pl.BlockSpec(array.shape, lambda i: (0, 0))
    in_specs = [flat] + ([whole(own)] if first else [flat, stat, stat]) + [whole(b) for b in blocks]
    operands = [queries] + ([own] if first else list(state)) + list(blocks)
    if last:
        out_specs = flat
        out_shape = jax.ShapeDtypeStruct((rows, width), jnp.bfloat16)
    else:
        out_specs = [flat, stat, stat]
        out_shape = [jax.ShapeDtypeStruct((rows, width), jnp.float32)] + [
            jax.ShapeDtypeStruct((heads, rows, 1), jnp.float32)
        ] * 2
    keys = sum(b.shape[0] for b in blocks) + (own.shape[0] if first else 0)
    return pl.pallas_call(
        functools.partial(attend_kernel, first, last, head_size),
        grid=(heads // HEADS_AT_ONCE,),
        in_specs=in_specs,
        out_specs=out_specs,
        out_shape=out_shape,
        cost_estimate=pl.CostEstimate(
            flops=4 * rows * width * keys,
            bytes_accessed=2 * keys * 2 * head_size + 8 * rows * width,
            transcendentals=rows * heads * keys,
        ),
        compiler_params=pltpu.CompilerParams(vmem_limit_bytes=32 * 1024 * 1024),
    )(*operands)


def choose_prefix(own, owners, sizes):
    groups, members = sizes
    group_index = lax.axis_index("group")
    member_index = lax.axis_index("member")
    wanted = pick_value(owners, group_index)
    if groups != 4:
        every_block = lax.all_gather(own, "group", axis=0)
        return lax.dynamic_index_in_dim(every_block, wanted, 0, keepdims=False)
    near = 1 + member_index % 2
    far = 3 - near

    def step(block, flip):
        pairs = [
            (g * members + m, (g ^ (flip ^ (3 * (m % 2)))) * members + m)
            for g in range(groups)
            for m in range(members)
        ]
        return lax.ppermute(block, ("group", "member"), pairs)

    beside = step(own, 1)
    wanted_there = pick_value(owners, group_index ^ far)
    passed = jnp.where(wanted_there == (group_index ^ near), beside, own)
    across = step(passed, 2)
    return jnp.where(
        wanted == group_index, own, jnp.where(wanted == (group_index ^ near), beside, across)
    )


def shards(
    sizes,
    activations,
    lengths,
    assignment,
    owners,
    prefix_cache,
    first_gain,
    first_bias,
    query_weight,
    keyval_weight,
    output_weight,
    second_gain,
    second_bias,
    expand_weight,
    contract_weight,
):
    groups, members = sizes
    chips = members // 2
    order = ring_order(chips)
    after = {order[i]: order[(i + 1) % chips] for i in range(chips)}
    ring_pairs = [(2 * z + c, 2 * after[z] + c) for z in range(chips) for c in range(2)]
    swap_pairs = [(m, m ^ 1) for m in range(members)]
    ring = lambda block: lax.ppermute(block, "member", ring_pairs)
    swap = lambda block: lax.ppermute(block, "member", swap_pairs)

    member_index = lax.axis_index("member")
    request = pick_value(assignment[0], member_index)
    length_here = pick_value(lengths[0], request)
    tokens = activations[0]
    row_count = tokens.shape[0]
    head_size = prefix_cache.shape[2] // 2

    block = choose_prefix(prefix_cache[0], owners, sizes)
    expand_other = swap(expand_weight)
    contract_other = swap(contract_weight)

    tokens_wide = tokens.astype(jnp.float32)
    normed = layer_norm(tokens_wide, first_gain, first_bias).astype(jnp.bfloat16)
    queries = jnp.dot(normed, query_weight, preferred_element_type=jnp.float32).astype(jnp.bfloat16)
    keys_values = jnp.dot(normed, keyval_weight, preferred_element_type=jnp.float32).astype(
        jnp.bfloat16
    )

    state = None
    for step in range(chips):
        later = ring(block) if step < chips - 1 else None
        other = swap(block)
        state = attend(queries, keys_values, state, [block, other], step == chips - 1, head_size)
        block = later
    attended = state

    residual = tokens_wide + jnp.dot(attended, output_weight, preferred_element_type=jnp.float32)
    second = layer_norm(residual, second_gain, second_bias).astype(jnp.bfloat16)

    def feed_forward(rows):
        total = None
        for expand, contract in ((expand_weight, contract_weight), (expand_other, contract_other)):
            hidden = jax.nn.gelu(
                jnp.dot(rows, expand, preferred_element_type=jnp.float32), approximate=True
            ).astype(jnp.bfloat16)
            part = jnp.dot(hidden, contract, preferred_element_type=jnp.float32)
            total = part if total is None else total + part
        return total

    rows, summed = second, None
    for step in range(1, chips):
        rows = ring(rows)
        part = feed_forward(rows)
        part = part if summed is None else part + summed.astype(jnp.float32)
        summed = ring(part.astype(jnp.bfloat16))
    total = residual + feed_forward(second) + summed.astype(jnp.float32)
    is_live = lax.broadcasted_iota(jnp.int32, (row_count, 1), 0) < length_here
    return jnp.where(is_live, total, 0.0).astype(jnp.bfloat16)[None]


def solution(mesh):
    sizes = (mesh.shape["group"], mesh.shape["member"])
    return jax.shard_map(
        functools.partial(shards, sizes),
        mesh=mesh,
        in_specs=(
            P("group", "member", None),
            P("group", None),
            P("group", None),
            P(),
            P("group", "member", None),
            P(),
            P(),
            P(),
            P(),
            P(),
            P(),
            P(),
            P(None, "member"),
            P("member", None),
        ),
        out_specs=P("group", "member", None),
        check_vma=False,
    )
```

time: 288 us -> 196 us (0.68)
  waiting for transfers between devices: 167 us -> 66.3 us
  Pallas kernels: 0 us -> 44.8 us
  starting transfers between devices: 0.31 us -> 19.4 us
  other arithmetic: 22.2 us -> 8.13 us
  between operations: 15.2 us -> 2.18 us
  matrix products: 67.1 us -> 55 us
  local copies, waits for them, and re-layouts: 8.7 us -> 0.06 us
  loops' own time: 5.68 us -> 0 us
    all_gather x3 -> x0, waiting for transfers between devices: 121 us -> none  [the longest x1 45.8 us: shards(): lax.all_gather(second, 'member', axis=0, tiled=True)]
    ppermute x0 -> x17, waiting for transfers between devices: none -> 66.3 us  [the longest x9 55.1 us: shards(): ring = lambda block: lax.ppermute(block, 'member', ring_pairs)]
    reduce_scatter x1 -> x0, waiting for transfers between devices: 45.8 us -> none  [shards(): lax.psum_scatter(jnp.dot(hidden, contract_weight, preferred_element_type=...]
    pallas_call x0 -> x4, Pallas kernels: none -> 44.8 us  [attend(): pl.pallas_call(functools.partial(attend_kernel, first, last, head_size),...]
    ppermute x0 -> x17, starting transfers between devices: none -> 19.4 us  [the longest x9 13.1 us: shards(): ring = lambda block: lax.ppermute(block, 'member', ring_pairs)]
    reduce_sum x9 -> x0, other arithmetic: 11.1 us -> none  [the longest x8 11 us: advance(): denominator_next = denominator_now * rescale + jnp.sum(exponent, axis=-1)]
    dot_general x19 -> x8, matrix products: 57 us -> 48.6 us  [feed_forward(): part = jnp.dot(hidden, contract, preferred_element_type=jnp.float32)]
    dynamic_slice x9 -> x0, local copies, waits for them, and re-layouts: 6.56 us -> none  [the longest x8 4.69 us: folded_attention(): lax.scan(advance, running, jnp.arange(extent // stride, dtype=jnp.int32))]
  transfers between devices with their start and end apart: 4 -> 17, of which waited for: 4 -> 10; matrix products, arithmetic and copies ran while one was open for 4% -> 25% of each run, Pallas kernels for 0% -> 23%
where the time goes in v1:
time: 196 us
  waiting for transfers between devices  66.3 us (34%)
  matrix products  55 us (28%)
  Pallas kernels  44.8 us (23%)
  starting transfers between devices  19.4 us (10%)
  other arithmetic  8.13 us (4%)
  between operations  2.18 us (1%)
    ppermute x9, waiting for transfers between devices, shards(): ring = lambda block: lax.ppermute(block, 'member', ring_pairs)  55.1 us
    dot_general x8, matrix products, feed_forward(): part = jnp.dot(hidden, contract, preferred_element_type=jnp.float32)  48.6 us
    pallas_call x4, Pallas kernels, attend(): pl.pallas_call(functools.partial(attend_kernel, first, last, head_size),...  44.8 us
    ppermute x9, starting transfers between devices, shards(): ring = lambda block: lax.ppermute(block, 'member', ring_pairs)  13.1 us
    ppermute x2, waiting for transfers between devices, step(): return lax.ppermute(block, ('group', 'member'), pairs)  11.3 us
    ppermute x2, starting transfers between devices, step(): return lax.ppermute(block, ('group', 'member'), pairs)  5.12 us
    dot_general x1, matrix products, shards(): jnp.dot(normed, query_weight, preferred_element_type=jnp.float32)  4.7 us
  transfers between devices with their start and end apart: 17, of which 10 were waited for; matrix products, arithmetic and copies ran while one was open for 25% of the time, Pallas kernels for 23%

profile of v1, /device:TPU:0, one launch (start us, length us, event | category | flops | bytes accessed | tf_op | source)
XLA Modules:
  0.0 195.9 jit_solution(4962600577134018432)
XLA Ops:
  0.0 3.0 %collective-permute-start = (bf16[1024,256]{1,0:T(8,128)(2,1)}, bf16[1024,256]{1,0:T(8,128)(2,1)S(1)}, u32[]{:S(2)}, u32[]{:S(2)}) collective-permute-start(bf16[1024,256]{1,0:T(8,128)(2,1)} %bitcast.59), channel_id=1, source_target_pairs={{0,8},{1,17},{2,10},{3,19},{4,12},{5,21},{6,14},{7,23},{8,0},{9,25... | collective-permute-start | bytes 1572872 | tf_op jit(solution)/shard_map/ppermute | solution.py:144
  5.0 5.4 %collective-permute-done = bf16[1024,256]{1,0:T(8,128)(2,1)S(1)} collective-permute-done((bf16[1024,256]{1,0:T(8,128)(2,1)}, bf16[1024,256]{1,0:T(8,128)(2,1)S(1)}, u32[]{:S(2)}, u32[]{:S(2)}) %collective-permute-start) | collective-permute-done | bytes 524320 | tf_op jit(solution)/shard_map/ppermute | solution.py:144
  14.9 5.9 %collective-permute-done.1 = bf16[1024,256]{1,0:T(8,128)(2,1)S(1)} collective-permute-done((bf16[1024,256]{1,0:T(8,128)(2,1)S(1)}, bf16[1024,256]{1,0:T(8,128)(2,1)S(1)}, u32[]{:S(2)}, u32[]{:S(2)}) %collective-permute-start.1) | collective-permute-done | bytes 524320 | tf_op jit(solution)/shard_map/ppermute | solution.py:144
  25.7 9.5 %collective-permute-done.3.refs_4_ = bf16[1024,256]{1,0:T(8,128)(2,1)S(1)} collective-permute-done((bf16[1024,256]{1,0:T(8,128)(2,1)S(1)}, bf16[1024,256]{1,0:T(8,128)(2,1)S(1)}, u32[]{:S(2)}, u32[]{:S(2)}) %collective-permute-start.3) | collective-permute-done | bytes 524320 | tf_op jit(solution)/shard_map/ppermute | solution.py:178
  37.0 10.5 %collective-permute-done.5.refs_4_ = bf16[1024,256]{1,0:T(8,128)(2,1)S(1)} collective-permute-done((bf16[1024,256]{1,0:T(8,128)(2,1)S(1)}, bf16[1024,256]{1,0:T(8,128)(2,1)S(1)}, u32[]{:S(2)}, u32[]{:S(2)}) %collective-permute-start.5) | collective-permute-done | bytes 524320 | tf_op jit(solution)/shard_map/ppermute | solution.py:178
  48.2 4.7 %convolution_convert_fusion.refs_0_ = bf16[128,2048]{1,0:T(8,128)(2,1)S(1)} fusion(bf16[2048,2048]{1,0:T(8,128)(2,1)} %param.21, bf16[1,128,2048]{2,1,0:T(8,128)(2,1)S(1)} %copy-done.1, f32[2048]{0:T(1024)S(1)} %copy-done.4, f32[2048]{0:T(1024)S(1)} %copy-done.5, f32[128]{0:T(128)S(1)} %add_rsqrt_fusion.1, f32[128]{0:T(128)S(1)} %broadcast_multiply_fusion.1), kind=kOutput, calls=%fused_computation.10 | convolution fusion | flops 1075576832 | bytes 9454592 | tf_op jit(solution)/shard_map/dot_general | solution.py:194
  53.4 5.4 %collective-permute-done.7.refs_4_ = bf16[1024,256]{1,0:T(8,128)(2,1)S(1)} collective-permute-done((bf16[1024,256]{1,0:T(8,128)(2,1)S(1)}, bf16[1024,256]{1,0:T(8,128)(2,1)S(1)}, u32[]{:S(2)}, u32[]{:S(2)}) %collective-permute-start.7) | collective-permute-done | bytes 524320 | tf_op jit(solution)/shard_map/ppermute | solution.py:178
  58.8 11.2 %shard_map.136 = (f32[128,2048]{1,0:T(8,128)S(1)}, f32[16,128,1]{2,1,0:T(8,128)S(1)}, f32[16,128,1]{2,1,0:T(8,128)S(1)}) custom-call(bf16[128,2048]{1,0:T(8,128)(2,1)S(1)} %convolution_convert_fusion.refs_0_, bf16[128,256]{1,0:T(8,128)(2,1)S(1)} %convolution_convert_fusion.1.refs_1_, bf16[1024,256]{1,0:T(8,128)(2,1)S(1)} %select_select_fusion.refs_2_, ...), custom_call_target="tpu_custom_call" | custom-call | flops 2281701376 | bytes 3211264 | tf_op jit(solution)/shard_map/pallas_call | solution.py:112
  69.9 11.1 %shard_map.137 = (f32[128,2048]{1,0:T(8,128)S(1)}, f32[16,128,1]{2,1,0:T(8,128)S(1)}, f32[16,128,1]{2,1,0:T(8,128)S(1)}) custom-call(bf16[128,2048]{1,0:T(8,128)(2,1)S(1)} %convolution_convert_fusion.refs_0_, f32[128,2048]{1,0:T(8,128)S(1)} %get-tuple-element.14.refs_1_, f32[16,128,1]{2,1,0:T(8,128)S(1)} %get-tuple-element.15.refs_2_, ...), custom_call_target="tpu_custom_call" | custom-call | flops 2147483648 | bytes 3145728 | tf_op jit(solution)/shard_map/pallas_call | solution.py:112
  81.1 11.1 %shard_map.138 = (f32[128,2048]{1,0:T(8,128)S(1)}, f32[16,128,1]{2,1,0:T(8,128)S(1)}, f32[16,128,1]{2,1,0:T(8,128)S(1)}) custom-call(bf16[128,2048]{1,0:T(8,128)(2,1)S(1)} %convolution_convert_fusion.refs_0_, f32[128,2048]{1,0:T(8,128)S(1)} %get-tuple-element.17.refs_1_, f32[16,128,1]{2,1,0:T(8,128)S(1)} %get-tuple-element.18.refs_2_, ...), custom_call_target="tpu_custom_call" | custom-call | flops 2147483648 | bytes 3145728 | tf_op jit(solution)/shard_map/pallas_call | solution.py:112
  92.2 11.4 %shard_map.139 = bf16[128,2048]{1,0:T(8,128)(2,1)S(1)} custom-call(bf16[128,2048]{1,0:T(8,128)(2,1)S(1)} %convolution_convert_fusion.refs_0_, f32[128,2048]{1,0:T(8,128)S(1)} %get-tuple-element.20.refs_1_, f32[16,128,1]{2,1,0:T(8,128)S(1)} %get-tuple-element.21.refs_2_, f32[16,128,1]{2,1,0:T(8,128)S(1)} %get-tuple-element.22.refs_3_, ...), custom_call_target="tpu_custom_call" | custom-call | flops 2147483648 | bytes 3145728 | tf_op jit(solution)/shard_map/pallas_call | solution.py:112
  108.8 12.1 %collective-permute-done.11 = bf16[128,2048]{1,0:T(8,128)(2,1)S(1)} collective-permute-done((bf16[128,2048]{1,0:T(8,128)(2,1)S(1)}, bf16[128,2048]{1,0:T(8,128)(2,1)S(1)}, u32[]{:S(2)}, u32[]{:S(2)}) %collective-permute-start.11) | collective-permute-done | bytes 524320 | tf_op jit(solution)/shard_map/ppermute | solution.py:178
  121.4 6.0 %fusion.82 = f32[128,2048]{1,0:T(8,128)} fusion(bf16[1024,2048]{1,0:T(8,128)(2,1)} %param.27, bf16[128,2048]{1,0:T(8,128)(2,1)S(1)} %collective-permute-done.11, bf16[2048,1024]{1,0:T(8,128)(2,1)} %param.26), kind=kOutput, calls=%fused_computation.102 | convolution fusion | flops 1074921472 | bytes 9961472 | tf_op jit(solution)/shard_map/dot_general | solution.py:216
  127.4 6.0 %fusion.8 = bf16[128,2048]{1,0:T(8,128)(2,1)} fusion(f32[128,2048]{1,0:T(8,128)} %fusion.82, bf16[1024,2048]{1,0:T(8,128)(2,1)} %collective-permute-done.10, bf16[128,2048]{1,0:T(8,128)(2,1)S(1)} %collective-permute-done.11, bf16[2048,1024]{1,0:T(8,128)(2,1)} %collective-permute-done.9), kind=kOutput, calls=%fused_computation.14 | convolution fusion | flops 1075445760 | bytes 10485760 | tf_op jit(solution)/shard_map/dot_general | solution.py:216
  133.4 3.4 %collective-permute-start.14 = (bf16[128,2048]{1,0:T(8,128)(2,1)}, bf16[128,2048]{1,0:T(8,128)(2,1)}, u32[]{:S(2)}, u32[]{:S(2)}) collective-permute-start(bf16[128,2048]{1,0:T(8,128)(2,1)} %fusion.8), channel_id=1, source_target_pairs={{0,2},{1,3},{2,6},{3,7},{4,0},{5,1},{6,4},{7,5},{8,10},{9,11},{10,... | collective-permute-start | bytes 1572872 | tf_op jit(solution)/shard_map/ppermute | solution.py:178
  136.8 6.2 %fusion.85 = f32[128,2048]{1,0:T(8,128)} fusion(bf16[1024,2048]{1,0:T(8,128)(2,1)} %param.27, bf16[128,2048]{1,0:T(8,128)(2,1)} %collective-permute-done.12, bf16[2048,1024]{1,0:T(8,128)(2,1)} %param.26), kind=kOutput, calls=%fused_computation.103 | convolution fusion | flops 1074921472 | bytes 9961472 | tf_op jit(solution)/shard_map/dot_general | solution.py:216
  142.9 6.5 %collective-permute-done.14 = bf16[128,2048]{1,0:T(8,128)(2,1)} collective-permute-done((bf16[128,2048]{1,0:T(8,128)(2,1)}, bf16[128,2048]{1,0:T(8,128)(2,1)}, u32[]{:S(2)}, u32[]{:S(2)}) %collective-permute-start.14) | collective-permute-done | bytes 524320 | tf_op jit(solution)/shard_map/ppermute | solution.py:178
  149.5 6.3 %fusion.7 = bf16[128,2048]{1,0:T(8,128)(2,1)} fusion(f32[128,2048]{1,0:T(8,128)} %fusion.85, bf16[1024,2048]{1,0:T(8,128)(2,1)} %collective-permute-done.10, bf16[128,2048]{1,0:T(8,128)(2,1)} %collective-permute-done.14, bf16[128,2048]{1,0:T(8,128)(2,1)} %collective-permute-done.12, bf16[2048,1024]{1,0:T(8,128)(2,1)} %collective-permute-done.9), kind=kOutput, calls=%fused_computation.13 | convolution fusion | flops 1075970048 | bytes 11010048 | tf_op jit(solution)/shard_map/dot_general | solution.py:216
  160.7 6.0 %fusion.88 = f32[128,2048]{1,0:T(8,128)} fusion(bf16[1024,2048]{1,0:T(8,128)(2,1)} %param.27, bf16[128,2048]{1,0:T(8,128)(2,1)S(1)} %collective-permute-done.13, bf16[2048,1024]{1,0:T(8,128)(2,1)} %param.26), kind=kOutput, calls=%fused_computation.104 | convolution fusion | flops 1074921472 | bytes 9961472 | tf_op jit(solution)/shard_map/dot_general | solution.py:216
  166.7 3.6 %collective-permute-done.15 = bf16[128,2048]{1,0:T(8,128)(2,1)} collective-permute-done((bf16[128,2048]{1,0:T(8,128)(2,1)}, bf16[128,2048]{1,0:T(8,128)(2,1)}, u32[]{:S(2)}, u32[]{:S(2)}) %collective-permute-start.15) | collective-permute-done | bytes 524320 | tf_op jit(solution)/shard_map/ppermute | solution.py:178
  170.3 6.1 %fusion.6 = bf16[128,2048]{1,0:T(8,128)(2,1)} fusion(f32[128,2048]{1,0:T(8,128)} %fusion.88, bf16[1024,2048]{1,0:T(8,128)(2,1)} %collective-permute-done.10, bf16[128,2048]{1,0:T(8,128)(2,1)} %collective-permute-done.15, bf16[128,2048]{1,0:T(8,128)(2,1)S(1)} %collective-permute-done.13, bf16[2048,1024]{1,0:T(8,128)(2,1)} %collective-permute-done.9), kind=kOutput, calls=%fused_computation.12 | convolution fusion | flops 1075970048 | bytes 11010048 | tf_op jit(solution)/shard_map/dot_general | solution.py:216
  178.9 6.0 %fusion.91 = f32[128,2048]{1,0:T(8,128)} fusion(bf16[1024,2048]{1,0:T(8,128)(2,1)} %param.27, bf16[128,2048]{1,0:T(8,128)(2,1)S(1)} %add_convert_fusion, bf16[2048,1024]{1,0:T(8,128)(2,1)} %param.26), kind=kOutput, calls=%fused_computation.105 | convolution fusion | flops 1074921472 | bytes 9961472 | tf_op jit(solution)/shard_map/dot_general | solution.py:216
  184.9 4.9 %collective-permute-done.16 = bf16[128,2048]{1,0:T(8,128)(2,1)S(1)} collective-permute-done((bf16[128,2048]{1,0:T(8,128)(2,1)}, bf16[128,2048]{1,0:T(8,128)(2,1)S(1)}, u32[]{:S(2)}, u32[]{:S(2)}) %collective-permute-start.16) | collective-permute-done | bytes 524320 | tf_op jit(solution)/shard_map/ppermute | solution.py:178
  189.8 6.1 %fusion.9 = bf16[1,128,2048]{2,1,0:T(8,128)(2,1)} fusion(f32[128,2048]{1,0:T(8,128)S(1)} %get-tuple-element.26, f32[128,2048]{1,0:T(8,128)} %fusion.91, bf16[1024,2048]{1,0:T(8,128)(2,1)} %collective-permute-done.10, bf16[128,2048]{1,0:T(8,128)(2,1)S(1)} %collective-permute-done.16, pred[128]{0:T(512)(128)(4,1)S(1)} %iota_compare_fusion, ...), kind=kOutput, calls=%fused_computation.15 | convolution fusion | flops 1076494336 | bytes 12058752 | tf_op jit(solution)/shard_map/dot_general | solution.py:216
  (60 shorter events, 25.4 us)
Async XLA Ops:
  0.0 53.0 %copy-start = (bf16[2048,256]{1,0:T(8,128)(2,1)S(1)}, bf16[2048,256]{1,0:T(8,128)(2,1)}, u32[]{:S(2)}) copy-start(bf16[2048,256]{1,0:T(8,128)(2,1)} %param.22) | copy-start | bytes 3145732
  0.0 36.1 %copy-start.1 = (bf16[1,128,2048]{2,1,0:T(8,128)(2,1)S(1)}, bf16[1,128,2048]{2,1,0:T(8,128)(2,1)}, u32[]{:S(2)}) copy-start(bf16[1,128,2048]{2,1,0:T(8,128)(2,1)} %param.14) | copy-start | bytes 1572868
  0.0 48.2 %copy-start.5 = (f32[2048]{0:T(1024)S(1)}, f32[2048]{0:T(1024)}, u32[]{:S(2)}) copy-start(f32[2048]{0:T(1024)} %param.19) | copy-start | bytes 24580
  0.0 48.2 %copy-start.4 = (f32[2048]{0:T(1024)S(1)}, f32[2048]{0:T(1024)}, u32[]{:S(2)}) copy-start(f32[2048]{0:T(1024)} %param.20) | copy-start | bytes 24580
  0.0 10.4 %collective-permute-start = (bf16[1024,256]{1,0:T(8,128)(2,1)}, bf16[1024,256]{1,0:T(8,128)(2,1)S(1)}, u32[]{:S(2)}, u32[]{:S(2)}) collective-permute-start(bf16[1024,256]{1,0:T(8,128)(2,1)} %bitcast.59), channel_id=1, source_target_pairs={{0,8},{1,17},{2,10},{3,19},{4,12},{5,21},{6,14},{7,23},{8,0},{9,25... | collective-permute-start | bytes 1572872 | tf_op jit(solution)/shard_map/ppermute | solution.py:144
  11.5 9.3 %collective-permute-start.1 = (bf16[1024,256]{1,0:T(8,128)(2,1)S(1)}, bf16[1024,256]{1,0:T(8,128)(2,1)S(1)}, u32[]{:S(2)}, u32[]{:S(2)}) collective-permute-start(bf16[1024,256]{1,0:T(8,128)(2,1)S(1)} %broadcast_select_fusion), channel_id=1, source_target_pairs={{0,16},{1,9},{2,18},{3,11},{4,20},{5,13},{6,22},{7,15},{8,24},{9,1... | collective-permute-start | bytes 1572872 | tf_op jit(solution)/shard_map/ppermute | solution.py:144
  21.9 13.4 %collective-permute-start.3 = (bf16[1024,256]{1,0:T(8,128)(2,1)S(1)}, bf16[1024,256]{1,0:T(8,128)(2,1)S(1)}, u32[]{:S(2)}, u32[]{:S(2)}) collective-permute-start(bf16[1024,256]{1,0:T(8,128)(2,1)S(1)} %select_select_fusion.refs_2_), channel_id=1, source_target_pairs={{0,2},{1,3},{2,6},{3,7},{4,0},{5,1},{6,4},{7,5},{8,10},{9,11},{10,... | collective-permute-start | bytes 1572872 | tf_op jit(solution)/shard_map/ppermute | solution.py:178
  24.0 103.4 %collective-permute-start.10 = (bf16[1024,2048]{1,0:T(8,128)(2,1)}, bf16[1024,2048]{1,0:T(8,128)(2,1)}, u32[]{:S(2)}, u32[]{:S(2)}) collective-permute-start(bf16[1024,2048]{1,0:T(8,128)(2,1)} %param.27), channel_id=1, source_target_pairs={{0,1},{1,0},{2,3},{3,2},{4,5},{5,4},{6,7},{7,6},{8,9},{9,8},{10,11... | collective-permute-start | bytes 12582920 | tf_op jit(solution)/shard_map/ppermute | solution.py:179
  24.0 103.4 %collective-permute-start.9 = (bf16[2048,1024]{1,0:T(8,128)(2,1)}, bf16[2048,1024]{1,0:T(8,128)(2,1)}, u32[]{:S(2)}, u32[]{:S(2)}) collective-permute-start(bf16[2048,1024]{1,0:T(8,128)(2,1)} %param.26), channel_id=1, source_target_pairs={{0,1},{1,0},{2,3},{3,2},{4,5},{5,4},{6,7},{7,6},{8,9},{9,8},{10,11... | collective-permute-start | bytes 12582920 | tf_op jit(solution)/shard_map/ppermute | solution.py:179
  35.3 12.2 %collective-permute-start.5 = (bf16[1024,256]{1,0:T(8,128)(2,1)S(1)}, bf16[1024,256]{1,0:T(8,128)(2,1)S(1)}, u32[]{:S(2)}, u32[]{:S(2)}) collective-permute-start(bf16[1024,256]{1,0:T(8,128)(2,1)S(1)} %collective-permute-done.3.refs_4_), channel_id=1, source_target_pairs={{0,2},{1,3},{2,6},{3,7},{4,0},{5,1},{6,4},{7,5},{8,10},{9,11},{10,... | collective-permute-start | bytes 1572872 | tf_op jit(solution)/shard_map/ppermute | solution.py:178
  36.4 16.5 %collective-permute-start.2 = (bf16[1024,256]{1,0:T(8,128)(2,1)S(1)}, bf16[1024,256]{1,0:T(8,128)(2,1)S(1)}, u32[]{:S(2)}, u32[]{:S(2)}) collective-permute-start(bf16[1024,256]{1,0:T(8,128)(2,1)S(1)} %select_select_fusion.refs_2_), channel_id=1, source_target_pairs={{0,1},{1,0},{2,3},{3,2},{4,5},{5,4},{6,7},{7,6},{8,9},{9,8},{10,11... | collective-permute-start | bytes 1572872 | tf_op jit(solution)/shard_map/ppermute | solution.py:179
  36.5 33.5 %collective-permute-start.4 = (bf16[1024,256]{1,0:T(8,128)(2,1)S(1)}, bf16[1024,256]{1,0:T(8,128)(2,1)S(1)}, u32[]{:S(2)}, u32[]{:S(2)}) collective-permute-start(bf16[1024,256]{1,0:T(8,128)(2,1)S(1)} %collective-permute-done.3.refs_4_), channel_id=1, source_target_pairs={{0,1},{1,0},{2,3},{3,2},{4,5},{5,4},{6,7},{7,6},{8,9},{9,8},{10,11... | collective-permute-start | bytes 1572872 | tf_op jit(solution)/shard_map/ppermute | solution.py:179
  47.5 11.3 %collective-permute-start.7 = (bf16[1024,256]{1,0:T(8,128)(2,1)S(1)}, bf16[1024,256]{1,0:T(8,128)(2,1)S(1)}, u32[]{:S(2)}, u32[]{:S(2)}) collective-permute-start(bf16[1024,256]{1,0:T(8,128)(2,1)S(1)} %collective-permute-done.5.refs_4_), channel_id=1, source_target_pairs={{0,2},{1,3},{2,6},{3,7},{4,0},{5,1},{6,4},{7,5},{8,10},{9,11},{10,... | collective-permute-start | bytes 1572872 | tf_op jit(solution)/shard_map/ppermute | solution.py:178
  52.9 28.2 %collective-permute-start.6 = (bf16[1024,256]{1,0:T(8,128)(2,1)S(1)}, bf16[1024,256]{1,0:T(8,128)(2,1)S(1)}, u32[]{:S(2)}, u32[]{:S(2)}) collective-permute-start(bf16[1024,256]{1,0:T(8,128)(2,1)S(1)} %collective-permute-done.5.refs_4_), channel_id=1, source_target_pairs={{0,1},{1,0},{2,3},{3,2},{4,5},{5,4},{6,7},{7,6},{8,9},{9,8},{10,11... | collective-permute-start | bytes 1572872 | tf_op jit(solution)/shard_map/ppermute | solution.py:179
  58.8 33.5 %collective-permute-start.8 = (bf16[1024,256]{1,0:T(8,128)(2,1)S(1)}, bf16[1024,256]{1,0:T(8,128)(2,1)S(1)}, u32[]{:S(2)}, u32[]{:S(2)}) collective-permute-start(bf16[1024,256]{1,0:T(8,128)(2,1)S(1)} %collective-permute-done.7.refs_4_), channel_id=1, source_target_pairs={{0,1},{1,0},{2,3},{3,2},{4,5},{5,4},{6,7},{7,6},{8,9},{9,8},{10,11... | collective-permute-start | bytes 1572872 | tf_op jit(solution)/shard_map/ppermute | solution.py:179
  81.1 22.6 %slice-start = ((s8[8388608]{0:T(1024)(128)(4,1)}), s8[4194304]{0:T(1024)(128)(4,1)S(1)}, s32[]{:S(2)}) async-start(s8[8388608]{0:T(1024)(128)(4,1)} %bitcast.57), calls=%async_computation | async-start | bytes 8388608
  92.2 11.5 %slice-start.1 = ((s8[8388608]{0:T(1024)(128)(4,1)}), s8[4194304]{0:T(1024)(128)(4,1)S(1)}, s32[]{:S(2)}) async-start(s8[8388608]{0:T(1024)(128)(4,1)} %bitcast.57), calls=%async_computation.1 | async-start | bytes 8388608
  103.7 3.1 %copy-start.7 = (s32[1,8]{1,0:T(1,128)S(1)}, s32[1,8]{1,0:T(1,128)}, u32[]{:S(2)}) copy-start(s32[1,8]{1,0:T(1,128)} %param.15) | copy-start | bytes 100
  105.7 15.3 %collective-permute-start.11 = (bf16[128,2048]{1,0:T(8,128)(2,1)S(1)}, bf16[128,2048]{1,0:T(8,128)(2,1)S(1)}, u32[]{:S(2)}, u32[]{:S(2)}) collective-permute-start(bf16[128,2048]{1,0:T(8,128)(2,1)S(1)} %add_convert_fusion), channel_id=1, source_target_pairs={{0,2},{1,3},{2,6},{3,7},{4,0},{5,1},{6,4},{7,5},{8,10},{9,11},{10,... | collective-permute-start | bytes 1572872 | tf_op jit(solution)/shard_map/ppermute | solution.py:178
  120.9 15.8 %collective-permute-start.12 = (bf16[128,2048]{1,0:T(8,128)(2,1)S(1)}, bf16[128,2048]{1,0:T(8,128)(2,1)}, u32[]{:S(2)}, u32[]{:S(2)}) collective-permute-start(bf16[128,2048]{1,0:T(8,128)(2,1)S(1)} %collective-permute-done.11), channel_id=1, source_target_pairs={{0,2},{1,3},{2,6},{3,7},{4,0},{5,1},{6,4},{7,5},{8,10},{9,11},{10,... | collective-permute-start | bytes 1572872 | tf_op jit(solution)/shard_map/ppermute | solution.py:178
  133.4 16.1 %collective-permute-start.14 = (bf16[128,2048]{1,0:T(8,128)(2,1)}, bf16[128,2048]{1,0:T(8,128)(2,1)}, u32[]{:S(2)}, u32[]{:S(2)}) collective-permute-start(bf16[128,2048]{1,0:T(8,128)(2,1)} %fusion.8), channel_id=1, source_target_pairs={{0,2},{1,3},{2,6},{3,7},{4,0},{5,1},{6,4},{7,5},{8,10},{9,11},{10,... | collective-permute-start | bytes 1572872 | tf_op jit(solution)/shard_map/ppermute | solution.py:178
  136.8 23.9 %collective-permute-start.13 = (bf16[128,2048]{1,0:T(8,128)(2,1)}, bf16[128,2048]{1,0:T(8,128)(2,1)S(1)}, u32[]{:S(2)}, u32[]{:S(2)}) collective-permute-start(bf16[128,2048]{1,0:T(8,128)(2,1)} %collective-permute-done.12), channel_id=1, source_target_pairs={{0,2},{1,3},{2,6},{3,7},{4,0},{5,1},{6,4},{7,5},{8,10},{9,11},{10,... | collective-permute-start | bytes 1572872 | tf_op jit(solution)/shard_map/ppermute | solution.py:178
  155.7 14.6 %collective-permute-start.15 = (bf16[128,2048]{1,0:T(8,128)(2,1)}, bf16[128,2048]{1,0:T(8,128)(2,1)}, u32[]{:S(2)}, u32[]{:S(2)}) collective-permute-start(bf16[128,2048]{1,0:T(8,128)(2,1)} %fusion.7), channel_id=1, source_target_pairs={{0,2},{1,3},{2,6},{3,7},{4,0},{5,1},{6,4},{7,5},{8,10},{9,11},{10,... | collective-permute-start | bytes 1572872 | tf_op jit(solution)/shard_map/ppermute | solution.py:178
  176.4 13.4 %collective-permute-start.16 = (bf16[128,2048]{1,0:T(8,128)(2,1)}, bf16[128,2048]{1,0:T(8,128)(2,1)S(1)}, u32[]{:S(2)}, u32[]{:S(2)}) collective-permute-start(bf16[128,2048]{1,0:T(8,128)(2,1)} %fusion.6), channel_id=1, source_target_pairs={{0,2},{1,3},{2,6},{3,7},{4,0},{5,1},{6,4},{7,5},{8,10},{9,11},{10,... | collective-permute-start | bytes 1572872 | tf_op jit(solution)/shard_map/ppermute | solution.py:178
  (3 other events, 5.8 us)

commit v2 on v1

v2 whole, which is shorter than its diff:
```python
import functools
import math

import jax
import jax.numpy as jnp
from jax import lax
from jax.experimental import pallas as pl
from jax.experimental.pallas import tpu as pltpu
from jax.sharding import PartitionSpec as P

EPSILON = 1e-05
NEGATIVE = -1e30
HEADS_AT_ONCE = 8
HEADS_STACKED = 2


def layer_norm(values, gain, bias):
    average = jnp.mean(values, axis=-1, keepdims=True)
    centered = values - average
    spread = jnp.mean(centered * centered, axis=-1, keepdims=True)
    return centered * lax.rsqrt(spread + EPSILON) * gain + bias


def pick_value(table, wanted):
    slots_at = lax.broadcasted_iota(jnp.int32, table.shape, 0)
    return jnp.sum(jnp.where(slots_at == wanted, table, 0))


def ring_order(chips):
    return list(range(0, 1)) + list(range(1, chips, 2)) + list(range(chips - 2 + chips % 2, 0, -2))


def attend_kernel(first, last, head_size, group, *refs):
    refs = list(refs)
    query_ref = refs.pop(0)
    if first:
        own_ref = refs.pop(0)
    else:
        weighted_in, highest_in, denominator_in = refs[:3]
        del refs[:3]
    outs = 1 if last else 3
    block_refs, out_refs = refs[:-outs], refs[-outs:]
    rows = query_ref.shape[0]
    heads = query_ref.shape[1] // head_size

    def stacked(ref, start):
        return jnp.concatenate(
            [ref[:, (start + h) * head_size : (start + h + 1) * head_size] for h in range(group)], axis=0
        )

    def all_scores(start):
        queries = stacked(query_ref, start)
        result = []
        for ref in ([own_ref] if first else []) + block_refs:
            scores = lax.dot_general(
                queries, ref[:, :head_size], (((1,), (1,)), ((), ())), preferred_element_type=jnp.float32
            )
            result.append(scores)
        if first:
            row_at = lax.broadcasted_iota(jnp.int32, result[0].shape, 0) % rows
            column_at = lax.broadcasted_iota(jnp.int32, result[0].shape, 1)
            result[0] = jnp.where(column_at <= row_at, result[0], NEGATIVE)
        return result

    def fold(start, scores):
        highest = None
        for part in scores:
            top = jnp.max(part, axis=-1, keepdims=True)
            highest = top if highest is None else jnp.maximum(highest, top)
        weighted, denominator = None, None
        if not first:
            before = jnp.concatenate([highest_in[start + h] for h in range(group)], axis=0)
            highest = jnp.maximum(highest, before)
            rescale = jnp.exp2(before - highest)
            weighted = stacked(weighted_in, start) * rescale
            denominator = (
                jnp.concatenate([denominator_in[start + h] for h in range(group)], axis=0) * rescale
            )
        for part, ref in zip(scores, ([own_ref] if first else []) + block_refs):
            exponent = jnp.exp2(part - highest)
            total = jnp.sum(exponent, axis=-1, keepdims=True)
            product = jnp.dot(
                exponent.astype(jnp.bfloat16), ref[:, head_size:], preferred_element_type=jnp.float32
            )
            weighted = product if weighted is None else weighted + product
            denominator = total if denominator is None else denominator + total
        if last:
            weighted = weighted / denominator
        for h in range(group):
            at = start + h
            part = slice(h * rows, (h + 1) * rows)
            out_refs[0][:, at * head_size : (at + 1) * head_size] = weighted[part].astype(out_refs[0].dtype)
            if not last:
                out_refs[1][at] = highest[part]
                out_refs[2][at] = denominator[part]

    scores = all_scores(0)
    for start in range(0, heads, group):
        following = all_scores(start + group) if start + group < heads else None
        fold(start, scores)
        scores = following


def attend(queries, own, state, blocks, last, head_size):
    rows, width = queries.shape
    heads = width // head_size
    at_once = math.gcd(heads, HEADS_AT_ONCE)
    wide = at_once * head_size
    first = state is None
    flat = pl.BlockSpec((rows, wide), lambda i: (0, i))
    stat = pl.BlockSpec((at_once, rows, 1), lambda i: (i, 0, 0))
    whole = lambda array: pl.BlockSpec(array.shape, lambda i: (0, 0))
    in_specs = [flat] + ([whole(own)] if first else [flat, stat, stat]) + [whole(b) for b in blocks]
    operands = [queries] + ([own] if first else list(state)) + list(blocks)
    if last:
        out_specs = flat
        out_shape = jax.ShapeDtypeStruct((rows, width), jnp.bfloat16)
    else:
        out_specs = [flat, stat, stat]
        out_shape = [jax.ShapeDtypeStruct((rows, width), jnp.float32)] + [
            jax.ShapeDtypeStruct((heads, rows, 1), jnp.float32)
        ] * 2
    keys = sum(b.shape[0] for b in blocks) + (own.shape[0] if first else 0)
    return pl.pallas_call(
        functools.partial(attend_kernel, first, last, head_size, math.gcd(at_once, HEADS_STACKED)),
        grid=(heads // at_once,),
        in_specs=in_specs,
        out_specs=out_specs,
        out_shape=out_shape,
        cost_estimate=pl.CostEstimate(
            flops=4 * rows * width * keys,
            bytes_accessed=2 * keys * 2 * head_size + 8 * rows * width,
            transcendentals=rows * heads * keys,
        ),
        compiler_params=pltpu.CompilerParams(vmem_limit_bytes=24 * 1024 * 1024),
    )(*operands)


def hold_kernel(count, *refs):
    sources, held, semaphores = refs[:count], refs[count:-1], refs[-1]
    copies = [
        pltpu.make_async_copy(sources[i], held[i], semaphores.at[i]) for i in range(count)
    ]
    for copy in copies:
        copy.start()
    for copy in copies:
        copy.wait()


def hold(*weights):
    count = len(weights)
    size = sum(w.size * w.dtype.itemsize for w in weights)
    return pl.pallas_call(
        functools.partial(hold_kernel, count),
        in_specs=[pl.BlockSpec(memory_space=pl.ANY)] * count,
        out_specs=[pl.BlockSpec(memory_space=pltpu.VMEM)] * count,
        out_shape=[pltpu.VMEM(w.shape, w.dtype) for w in weights],
        scratch_shapes=[pltpu.SemaphoreType.DMA((count,))],
        cost_estimate=pl.CostEstimate(flops=0, bytes_accessed=size, transcendentals=0),
        compiler_params=pltpu.CompilerParams(vmem_limit_bytes=4 * 1024 * 1024),
    )(*weights)


def feed_forward_kernel(count, rows_ref, *refs):
    expands, contracts, out_ref = refs[:count], refs[count:-1], refs[-1]
    total = None
    for expand_ref, contract_ref in zip(expands, contracts):
        extent = expand_ref.shape[1]
        stride = math.gcd(extent, 512)
        for start in range(0, extent, stride):
            hidden = jnp.dot(
                rows_ref[...], expand_ref[:, start : start + stride], preferred_element_type=jnp.float32
            )
            hidden = jax.nn.gelu(hidden, approximate=True).astype(jnp.bfloat16)
            part = jnp.dot(
                hidden, contract_ref[start : start + stride], preferred_element_type=jnp.float32
            )
            total = part if total is None else total + part
    out_ref[...] = total


def feed_forward(rows, expands, contracts):
    extent = sum(e.shape[1] for e in expands)
    return pl.pallas_call(
        functools.partial(feed_forward_kernel, len(expands)),
        in_specs=[pl.BlockSpec(memory_space=pltpu.VMEM)] * (1 + len(expands) + len(contracts)),
        out_specs=pl.BlockSpec(memory_space=pltpu.VMEM),
        out_shape=jax.ShapeDtypeStruct(rows.shape, jnp.float32),
        cost_estimate=pl.CostEstimate(
            flops=4 * rows.size * extent, bytes_accessed=6 * rows.size, transcendentals=rows.shape[0] * extent
        ),
        compiler_params=pltpu.CompilerParams(vmem_limit_bytes=16 * 1024 * 1024),
    )(rows, *expands, *contracts)


def choose_prefix(own, owners, sizes):
    groups, members = sizes
    group_index = lax.axis_index("group")
    member_index = lax.axis_index("member")
    wanted = pick_value(owners, group_index)
    if groups != 4:
        every_block = lax.all_gather(own, "group", axis=0)
        return lax.dynamic_index_in_dim(every_block, wanted, 0, keepdims=False)
    near = 1 + member_index % 2
    far = 3 - near

    def step(block, flip):
        pairs = [
            (g * members + m, (g ^ (flip ^ (3 * (m % 2)))) * members + m)
            for g in range(groups)
            for m in range(members)
        ]
        return lax.ppermute(block, ("group", "member"), pairs)

    beside = step(own, 1)
    wanted_there = pick_value(owners, group_index ^ far)
    passed = jnp.where(wanted_there == (group_index ^ near), beside, own)
    across = step(passed, 2)
    return jnp.where(
        wanted == group_index, own, jnp.where(wanted == (group_index ^ near), beside, across)
    )


def shards(
    sizes,
    activations,
    lengths,
    assignment,
    owners,
    prefix_cache,
    first_gain,
    first_bias,
    query_weight,
    keyval_weight,
    output_weight,
    second_gain,
    second_bias,
    expand_weight,
    contract_weight,
):
    groups, members = sizes
    chips = members // 2
    order = ring_order(chips)
    after = {order[i]: order[(i + 1) % chips] for i in range(chips)}
    ring_pairs = [(2 * z + c, 2 * after[z] + c) for z in range(chips) for c in range(2)]
    swap_pairs = [(m, m ^ 1) for m in range(members)]
    ring = lambda block: lax.ppermute(block, "member", ring_pairs)
    swap = lambda block: lax.ppermute(block, "member", swap_pairs)

    member_index = lax.axis_index("member")
    request = pick_value(assignment[0], member_index)
    length_here = pick_value(lengths[0], request)
    tokens = activations[0]
    row_count = tokens.shape[0]
    head_size = prefix_cache.shape[2] // 2

    block = choose_prefix(prefix_cache[0], owners, sizes)
    expand_other = swap(expand_weight)
    contract_other = swap(contract_weight)

    tokens_wide = tokens.astype(jnp.float32)
    normed = layer_norm(tokens_wide, first_gain, first_bias).astype(jnp.bfloat16)
    factor = math.log2(math.e) / math.sqrt(head_size)
    queries = jnp.dot(normed, query_weight, preferred_element_type=jnp.float32)
    queries = (queries * factor).astype(jnp.bfloat16)
    keys_values = jnp.dot(normed, keyval_weight, preferred_element_type=jnp.float32).astype(
        jnp.bfloat16
    )

    expand_here, contract_here = hold(expand_weight, contract_weight)
    block, queries, keys_values, expand_other, contract_other = lax.optimization_barrier(
        (block, queries, keys_values, expand_other, contract_other)
    )

    state = None
    for step in range(chips):
        last = step == chips - 1
        later = None if last else ring(block)
        other = swap(block)
        state = attend(queries, keys_values, state, [block], False, head_size)
        state = attend(queries, keys_values, state, [other], last, head_size)
        if step == 0:
            expand_other, contract_other = hold(expand_other, contract_other)
        if not last:
            later, state = lax.optimization_barrier((later, state))
        block = later
    attended = state

    expands, contracts = (expand_here, expand_other), (contract_here, contract_other)
    residual = tokens_wide + jnp.dot(attended, output_weight, preferred_element_type=jnp.float32)
    second = layer_norm(residual, second_gain, second_bias).astype(jnp.bfloat16)

    rows, summed = second, None
    for step in range(1, chips):
        rows = ring(rows)
        if step == 1:
            here = feed_forward(second, expands, contracts)
        part = feed_forward(rows, expands, contracts)
        part = part if summed is None else part + summed.astype(jnp.float32)
        summed = ring(part.astype(jnp.bfloat16))
    total = residual + here + summed.astype(jnp.float32)
    is_live = lax.broadcasted_iota(jnp.int32, (row_count, 1), 0) < length_here
    return jnp.where(is_live, total, 0.0).astype(jnp.bfloat16)[None]


def solution(mesh):
    sizes = (mesh.shape["group"], mesh.shape["member"])
    return jax.shard_map(
        functools.partial(shards, sizes),
        mesh=mesh,
        in_specs=(
            P("group", "member", None),
            P("group", None),
            P("group", None),
            P(),
            P("group", "member", None),
            P(),
            P(),
            P(),
            P(),
            P(),
            P(),
            P(),
            P(None, "member"),
            P("member", None),
        ),
        out_specs=P("group", "member", None),
        check_vma=False,
    )
```

time: 196 us -> 156 us (0.80)
  matrix products: 55 us -> 7.75 us
  waiting for transfers between devices: 66.3 us -> 72.2 us
  starting transfers between devices: 19.4 us -> 17.4 us
    dot_general x9 -> x1, matrix products: 53.3 us -> 4.95 us  [shards(): queries = jnp.dot(normed, query_weight, preferred_element_type=jnp.float32)]
    ppermute x9, waiting for transfers between devices: 55.1 us -> 69.7 us  [shards(): ring = lambda block: lax.ppermute(block, 'member', ring_pairs)]
    ppermute x2, waiting for transfers between devices: 11.3 us -> 2.41 us  [step(): return lax.ppermute(block, ('group', 'member'), pairs)]
    pallas_call x4 -> x14, Pallas kernels: 44.8 us -> 46 us  [the longest x8 30.2 us: attend(): pl.pallas_call(functools.partial(attend_kernel, first, last, head_size, m...]
  transfers between devices with their start and end apart: 17 -> 17, of which waited for: 10 -> 11; matrix products, arithmetic and copies ran while one was open for 25% -> 9% of each run, Pallas kernels for 23% -> 27%
where the time goes in v2:
time: 156 us
  waiting for transfers between devices  72.2 us (46%)
  Pallas kernels  46 us (29%)
  starting transfers between devices  17.4 us (11%)
  other arithmetic  9.6 us (6%)
  matrix products  7.75 us (5%)
  between operations  2.21 us (1%)
    ppermute x9, waiting for transfers between devices, shards(): ring = lambda block: lax.ppermute(block, 'member', ring_pairs)  69.7 us
    pallas_call x8, Pallas kernels, attend(): pl.pallas_call(functools.partial(attend_kernel, first, last, head_size, m...  30.2 us
    ppermute x9, starting transfers between devices, shards(): ring = lambda block: lax.ppermute(block, 'member', ring_pairs)  11.8 us
    pallas_call x4, Pallas kernels, feed_forward(): pl.pallas_call(functools.partial(feed_forward_kernel, len(expands)), in_s...  11.8 us
    ppermute x2, starting transfers between devices, step(): return lax.ppermute(block, ('group', 'member'), pairs)  5.04 us
    dot_general x1, matrix products, shards(): queries = jnp.dot(normed, query_weight, preferred_element_type=jnp.float32)  4.95 us
    pallas_call x2, Pallas kernels, hold(): pl.pallas_call(functools.partial(hold_kernel, count), in_specs=[pl.BlockS...  4.06 us
    reduce_sum x3, other arithmetic, pick_value(): return jnp.sum(jnp.where(slots_at == wanted, table, 0))  3.28 us
  transfers between devices with their start and end apart: 17, of which 11 were waited for; matrix products, arithmetic and copies ran while one was open for 9% of the time, Pallas kernels for 27%

profile of v2, /device:TPU:0, one launch (start us, length us, event | category | flops | bytes accessed | tf_op | source)
XLA Modules:
  0.0 155.9 jit_solution(7507532484823551333)
XLA Ops:
  14.1 4.9 %fusion.refs_0_ = bf16[128,2048]{1,0:T(8,128)(2,1)S(1)} fusion(bf16[2048,2048]{1,0:T(8,128)(2,1)} %param.21, bf16[1,128,2048]{2,1,0:T(8,128)(2,1)} %param.14, f32[2048]{0:T(1024)} %param.20, f32[2048]{0:T(1024)} %param.19, f32[128]{0:T(128)S(1)} %add_rsqrt_fusion.1, f32[128]{0:T(128)S(1)} %broadcast_multiply_fusion.1), kind=kOutput, calls=%fused_computation.2 | convolution fusion | flops 1075838976 | bytes 9454592 | tf_op jit(solution)/shard_map/dot_general | solution.py:264
  23.5 3.4 %shard_map.136 = (f32[128,2048]{1,0:T(8,128)S(1)}, f32[16,128,1]{2,1,0:T(8,128)S(1)}, f32[16,128,1]{2,1,0:T(8,128)S(1)}) custom-call(bf16[128,2048]{1,0:T(8,128)(2,1)S(1)} %fusion.refs_0_, bf16[128,256]{1,0:T(8,128)(2,1)S(1)} %convolution_convert_fusion.refs_1_, bf16[1024,256]{1,0:T(8,128)(2,1)S(1)} %select_select_fusion.refs_2_), custom_call_target="tpu_custom_call" | custom-call | flops 1207959552 | bytes 2686976 | tf_op jit(solution)/shard_map/pallas_call | solution.py:124
  26.9 3.7 %shard_map.137 = (f32[128,2048]{1,0:T(8,128)S(1)}, f32[16,128,1]{2,1,0:T(8,128)S(1)}, f32[16,128,1]{2,1,0:T(8,128)S(1)}) custom-call(bf16[128,2048]{1,0:T(8,128)(2,1)S(1)} %fusion.refs_0_, f32[128,2048]{1,0:T(8,128)S(1)} %get-tuple-element.50.refs_1_, f32[16,128,1]{2,1,0:T(8,128)S(1)} %get-tuple-element.51.refs_2_, ...), custom_call_target="tpu_custom_call" | custom-call | flops 1073741824 | bytes 2621440 | tf_op jit(solution)/shard_map/pallas_call | solution.py:124
  30.7 6.4 %collective-permute-done.4.refs_4_ = bf16[1024,256]{1,0:T(8,128)(2,1)S(1)} collective-permute-done((bf16[1024,256]{1,0:T(8,128)(2,1)S(1)}, bf16[1024,256]{1,0:T(8,128)(2,1)S(1)}, u32[]{:S(2)}, u32[]{:S(2)}) %collective-permute-start.4) | collective-permute-done | bytes 524320 | tf_op jit(solution)/shard_map/ppermute | solution.py:247
  37.9 3.7 %shard_map.138 = (f32[128,2048]{1,0:T(8,128)S(1)}, f32[16,128,1]{2,1,0:T(8,128)S(1)}, f32[16,128,1]{2,1,0:T(8,128)S(1)}) custom-call(bf16[128,2048]{1,0:T(8,128)(2,1)S(1)} %fusion.refs_0_, f32[128,2048]{1,0:T(8,128)S(1)} %get-tuple-element.57.refs_1_, f32[16,128,1]{2,1,0:T(8,128)S(1)} %get-tuple-element.58.refs_2_, ...), custom_call_target="tpu_custom_call" | custom-call | flops 1073741824 | bytes 2621440 | tf_op jit(solution)/shard_map/pallas_call | solution.py:124
  41.7 3.7 %shard_map.139 = (f32[128,2048]{1,0:T(8,128)S(1)}, f32[16,128,1]{2,1,0:T(8,128)S(1)}, f32[16,128,1]{2,1,0:T(8,128)S(1)}) custom-call(bf16[128,2048]{1,0:T(8,128)(2,1)S(1)} %fusion.refs_0_, f32[128,2048]{1,0:T(8,128)S(1)} %get-tuple-element.60.refs_1_, f32[16,128,1]{2,1,0:T(8,128)S(1)} %get-tuple-element.61.refs_2_, ...), custom_call_target="tpu_custom_call" | custom-call | flops 1073741824 | bytes 2621440 | tf_op jit(solution)/shard_map/pallas_call | solution.py:124
  45.4 6.9 %collective-permute-done.6.refs_4_ = bf16[1024,256]{1,0:T(8,128)(2,1)S(1)} collective-permute-done((bf16[1024,256]{1,0:T(8,128)(2,1)S(1)}, bf16[1024,256]{1,0:T(8,128)(2,1)S(1)}, u32[]{:S(2)}, u32[]{:S(2)}) %collective-permute-start.6) | collective-permute-done | bytes 524320 | tf_op jit(solution)/shard_map/ppermute | solution.py:247
  53.2 3.7 %shard_map.140 = (f32[128,2048]{1,0:T(8,128)S(1)}, f32[16,128,1]{2,1,0:T(8,128)S(1)}, f32[16,128,1]{2,1,0:T(8,128)S(1)}) custom-call(bf16[128,2048]{1,0:T(8,128)(2,1)S(1)} %fusion.refs_0_, f32[128,2048]{1,0:T(8,128)S(1)} %get-tuple-element.67.refs_1_, f32[16,128,1]{2,1,0:T(8,128)S(1)} %get-tuple-element.68.refs_2_, ...), custom_call_target="tpu_custom_call" | custom-call | flops 1073741824 | bytes 2621440 | tf_op jit(solution)/shard_map/pallas_call | solution.py:124
  56.9 3.7 %shard_map.141 = (f32[128,2048]{1,0:T(8,128)S(1)}, f32[16,128,1]{2,1,0:T(8,128)S(1)}, f32[16,128,1]{2,1,0:T(8,128)S(1)}) custom-call(bf16[128,2048]{1,0:T(8,128)(2,1)S(1)} %fusion.refs_0_, f32[128,2048]{1,0:T(8,128)S(1)} %get-tuple-element.70.refs_1_, f32[16,128,1]{2,1,0:T(8,128)S(1)} %get-tuple-element.71.refs_2_, ...), custom_call_target="tpu_custom_call" | custom-call | flops 1073741824 | bytes 2621440 | tf_op jit(solution)/shard_map/pallas_call | solution.py:124
  60.7 6.9 %collective-permute-done.8.refs_4_ = bf16[1024,256]{1,0:T(8,128)(2,1)S(1)} collective-permute-done((bf16[1024,256]{1,0:T(8,128)(2,1)S(1)}, bf16[1024,256]{1,0:T(8,128)(2,1)S(1)}, u32[]{:S(2)}, u32[]{:S(2)}) %collective-permute-start.8) | collective-permute-done | bytes 524320 | tf_op jit(solution)/shard_map/ppermute | solution.py:247
  67.6 3.7 %shard_map.142 = (f32[128,2048]{1,0:T(8,128)S(1)}, f32[16,128,1]{2,1,0:T(8,128)S(1)}, f32[16,128,1]{2,1,0:T(8,128)S(1)}) custom-call(bf16[128,2048]{1,0:T(8,128)(2,1)S(1)} %fusion.refs_0_, f32[128,2048]{1,0:T(8,128)S(1)} %get-tuple-element.76.refs_1_, f32[16,128,1]{2,1,0:T(8,128)S(1)} %get-tuple-element.77.refs_2_, ...), custom_call_target="tpu_custom_call" | custom-call | flops 1073741824 | bytes 2621440 | tf_op jit(solution)/shard_map/pallas_call | solution.py:124
  71.3 4.4 %shard_map.143 = bf16[128,2048]{1,0:T(8,128)(2,1)S(1)} custom-call(bf16[128,2048]{1,0:T(8,128)(2,1)S(1)} %fusion.refs_0_, f32[128,2048]{1,0:T(8,128)S(1)} %get-tuple-element.80.refs_1_, f32[16,128,1]{2,1,0:T(8,128)S(1)} %get-tuple-element.81.refs_2_, f32[16,128,1]{2,1,0:T(8,128)S(1)} %get-tuple-element.82.refs_3_, ...), custom_call_target="tpu_custom_call" | custom-call | flops 1073741824 | bytes 2621440 | tf_op jit(solution)/shard_map/pallas_call | solution.py:124
  79.8 3.5 %shard_map.145 = (bf16[2048,1024]{1,0:T(8,128)(2,1)S(1)}, bf16[1024,2048]{1,0:T(8,128)(2,1)S(1)}) custom-call(bf16[2048,1024]{1,0:T(8,128)(2,1)} %collective-permute-done.2.refs_0_, bf16[1024,2048]{1,0:T(8,128)(2,1)} %collective-permute-done.3.refs_1_), custom_call_target="tpu_custom_call" | custom-call | bytes 8388608 | tf_op jit(solution)/shard_map/pallas_call | solution.py:153
  83.3 9.7 %collective-permute-done.11.rows_ref = bf16[128,2048]{1,0:T(8,128)(2,1)S(1)} collective-permute-done((bf16[128,2048]{1,0:T(8,128)(2,1)S(1)}, bf16[128,2048]{1,0:T(8,128)(2,1)S(1)}, u32[]{:S(2)}, u32[]{:S(2)}) %collective-permute-start.11) | collective-permute-done | bytes 524320 | tf_op jit(solution)/shard_map/ppermute | solution.py:247
  93.8 2.9 %shard_map.149 = f32[128,2048]{1,0:T(8,128)S(1)} custom-call(bf16[128,2048]{1,0:T(8,128)(2,1)S(1)} %collective-permute-done.11.rows_ref, bf16[2048,1024]{1,0:T(8,128)(2,1)S(1)} %get-tuple-element.83.refs_0_, bf16[2048,1024]{1,0:T(8,128)(2,1)S(1)} %get-tuple-element.86.refs_1_, bf16[1024,2048]{1,0:T(8,128)(2,1)S(1)} %get-tuple-element.87.refs_2_, ...), custom_call_target="tpu_custom_call" | custom-call | flops 2147483648 | bytes 1572864 | tf_op jit(solution)/shard_map/pallas_call | solution.py:184
  96.8 3.6 %collective-permute-start.14 = (bf16[128,2048]{1,0:T(8,128)(2,1)S(1)}, bf16[128,2048]{1,0:T(8,128)(2,1)S(1)}, u32[]{:S(2)}, u32[]{:S(2)}) collective-permute-start(bf16[128,2048]{1,0:T(8,128)(2,1)S(1)} %convert_element_type.45), channel_id=1, source_target_pairs={{0,2},{1,3},{2,6},{3,7},{4,0},{5,1},{6,4},{7,5},{8,10},{9,11},{10,... | collective-permute-start | bytes 1572872 | tf_op jit(solution)/shard_map/ppermute | solution.py:247
  100.5 8.2 %collective-permute-done.12.rows_ref = bf16[128,2048]{1,0:T(8,128)(2,1)S(1)} collective-permute-done((bf16[128,2048]{1,0:T(8,128)(2,1)S(1)}, bf16[128,2048]{1,0:T(8,128)(2,1)S(1)}, u32[]{:S(2)}, u32[]{:S(2)}) %collective-permute-start.12) | collective-permute-done | bytes 524320 | tf_op jit(solution)/shard_map/ppermute | solution.py:247
  109.6 2.9 %shard_map.148 = f32[128,2048]{1,0:T(8,128)S(1)} custom-call(bf16[128,2048]{1,0:T(8,128)(2,1)S(1)} %collective-permute-done.12.rows_ref, bf16[2048,1024]{1,0:T(8,128)(2,1)S(1)} %get-tuple-element.83.refs_0_, bf16[2048,1024]{1,0:T(8,128)(2,1)S(1)} %get-tuple-element.86.refs_1_, bf16[1024,2048]{1,0:T(8,128)(2,1)S(1)} %get-tuple-element.87.refs_2_, ...), custom_call_target="tpu_custom_call" | custom-call | flops 2147483648 | bytes 1572864 | tf_op jit(solution)/shard_map/pallas_call | solution.py:184
  112.5 7.4 %collective-permute-done.14 = bf16[128,2048]{1,0:T(8,128)(2,1)S(1)} collective-permute-done((bf16[128,2048]{1,0:T(8,128)(2,1)S(1)}, bf16[128,2048]{1,0:T(8,128)(2,1)S(1)}, u32[]{:S(2)}, u32[]{:S(2)}) %collective-permute-start.14) | collective-permute-done | bytes 524320 | tf_op jit(solution)/shard_map/ppermute | solution.py:247
  121.0 10.2 %collective-permute-done.13.rows_ref = bf16[128,2048]{1,0:T(8,128)(2,1)S(1)} collective-permute-done((bf16[128,2048]{1,0:T(8,128)(2,1)S(1)}, bf16[128,2048]{1,0:T(8,128)(2,1)S(1)}, u32[]{:S(2)}, u32[]{:S(2)}) %collective-permute-start.13) | collective-permute-done | bytes 524320 | tf_op jit(solution)/shard_map/ppermute | solution.py:247
  131.2 2.9 %shard_map.147 = f32[128,2048]{1,0:T(8,128)S(1)} custom-call(bf16[128,2048]{1,0:T(8,128)(2,1)S(1)} %collective-permute-done.13.rows_ref, bf16[2048,1024]{1,0:T(8,128)(2,1)S(1)} %get-tuple-element.83.refs_0_, bf16[2048,1024]{1,0:T(8,128)(2,1)S(1)} %get-tuple-element.86.refs_1_, bf16[1024,2048]{1,0:T(8,128)(2,1)S(1)} %get-tuple-element.87.refs_2_, ...), custom_call_target="tpu_custom_call" | custom-call | flops 2147483648 | bytes 1572864 | tf_op jit(solution)/shard_map/pallas_call | solution.py:184
  134.1 7.0 %collective-permute-done.15 = bf16[128,2048]{1,0:T(8,128)(2,1)S(1)} collective-permute-done((bf16[128,2048]{1,0:T(8,128)(2,1)S(1)}, bf16[128,2048]{1,0:T(8,128)(2,1)S(1)}, u32[]{:S(2)}, u32[]{:S(2)}) %collective-permute-start.15) | collective-permute-done | bytes 524320 | tf_op jit(solution)/shard_map/ppermute | solution.py:247
  144.9 2.9 %shard_map.146 = f32[128,2048]{1,0:T(8,128)S(1)} custom-call(bf16[128,2048]{1,0:T(8,128)(2,1)S(1)} %add_convert_fusion.2.rows_ref, bf16[2048,1024]{1,0:T(8,128)(2,1)S(1)} %get-tuple-element.83.refs_0_, bf16[2048,1024]{1,0:T(8,128)(2,1)S(1)} %get-tuple-element.86.refs_1_, bf16[1024,2048]{1,0:T(8,128)(2,1)S(1)} %get-tuple-element.87.refs_2_, ...), custom_call_target="tpu_custom_call" | custom-call | flops 2147483648 | bytes 1572864 | tf_op jit(solution)/shard_map/pallas_call | solution.py:184
  147.9 7.0 %collective-permute-done.16 = bf16[128,2048]{1,0:T(8,128)(2,1)S(1)} collective-permute-done((bf16[128,2048]{1,0:T(8,128)(2,1)S(1)}, bf16[128,2048]{1,0:T(8,128)(2,1)S(1)}, u32[]{:S(2)}, u32[]{:S(2)}) %collective-permute-start.16) | collective-permute-done | bytes 524320 | tf_op jit(solution)/shard_map/ppermute | solution.py:247
  (70 shorter events, 29.9 us)
Async XLA Ops:
  0.0 9.1 %copy-start = (bf16[2048,256]{1,0:T(8,128)(2,1)S(1)}, bf16[2048,256]{1,0:T(8,128)(2,1)}, u32[]{:S(2)}) copy-start(bf16[2048,256]{1,0:T(8,128)(2,1)} %param.22) | copy-start | bytes 3145732
  0.0 21.3 %collective-permute-start.2 = (bf16[2048,1024]{1,0:T(8,128)(2,1)}, bf16[2048,1024]{1,0:T(8,128)(2,1)}, u32[]{:S(2)}, u32[]{:S(2)}) collective-permute-start(bf16[2048,1024]{1,0:T(8,128)(2,1)} %refs_0_.1), channel_id=1, source_target_pairs={{0,1},{1,0},{2,3},{3,2},{4,5},{5,4},{6,7},{7,6},{8,9},{9,8},{10,11... | collective-permute-start | bytes 12582920 | tf_op jit(solution)/shard_map/ppermute | solution.py:248
  0.5 20.9 %collective-permute-start.3 = (bf16[1024,2048]{1,0:T(8,128)(2,1)}, bf16[1024,2048]{1,0:T(8,128)(2,1)}, u32[]{:S(2)}, u32[]{:S(2)}) collective-permute-start(bf16[1024,2048]{1,0:T(8,128)(2,1)} %refs_1_.1), channel_id=1, source_target_pairs={{0,1},{1,0},{2,3},{3,2},{4,5},{5,4},{6,7},{7,6},{8,9},{9,8},{10,11... | collective-permute-start | bytes 12582920 | tf_op jit(solution)/shard_map/ppermute | solution.py:248
  0.5 10.3 %collective-permute-start = (bf16[1024,256]{1,0:T(8,128)(2,1)}, bf16[1024,256]{1,0:T(8,128)(2,1)S(1)}, u32[]{:S(2)}, u32[]{:S(2)}) collective-permute-start(bf16[1024,256]{1,0:T(8,128)(2,1)} %bitcast.35), channel_id=1, source_target_pairs={{0,8},{1,17},{2,10},{3,19},{4,12},{5,21},{6,14},{7,23},{8,0},{9,25... | collective-permute-start | bytes 1572872 | tf_op jit(solution)/shard_map/ppermute | solution.py:213
  11.9 9.3 %copy-start.5 = (bf16[1,1024,256]{2,1,0:T(8,128)(2,1)S(1)}, bf16[1,1024,256]{2,1,0:T(8,128)(2,1)}, u32[]{:S(2)}) copy-start(bf16[1,1024,256]{2,1,0:T(8,128)(2,1)} %param.18) | copy-start | bytes 1572868
  11.9 9.3 %collective-permute-start.1 = (bf16[1024,256]{1,0:T(8,128)(2,1)S(1)}, bf16[1024,256]{1,0:T(8,128)(2,1)S(1)}, u32[]{:S(2)}, u32[]{:S(2)}) collective-permute-start(bf16[1024,256]{1,0:T(8,128)(2,1)S(1)} %broadcast_select_fusion), channel_id=1, source_target_pairs={{0,16},{1,9},{2,18},{3,11},{4,20},{5,13},{6,22},{7,15},{8,24},{9,1... | collective-permute-start | bytes 1572872 | tf_op jit(solution)/shard_map/ppermute | solution.py:213
  21.3 5.6 %collective-permute-start.5 = (bf16[1024,256]{1,0:T(8,128)(2,1)S(1)}, bf16[1024,256]{1,0:T(8,128)(2,1)S(1)}, u32[]{:S(2)}, u32[]{:S(2)}) collective-permute-start(bf16[1024,256]{1,0:T(8,128)(2,1)S(1)} %select_select_fusion.refs_2_), channel_id=1, source_target_pairs={{0,1},{1,0},{2,3},{3,2},{4,5},{5,4},{6,7},{7,6},{8,9},{9,8},{10,11... | collective-permute-start | bytes 1572872 | tf_op jit(solution)/shard_map/ppermute | solution.py:248
  21.4 15.7 %collective-permute-start.4 = (bf16[1024,256]{1,0:T(8,128)(2,1)S(1)}, bf16[1024,256]{1,0:T(8,128)(2,1)S(1)}, u32[]{:S(2)}, u32[]{:S(2)}) collective-permute-start(bf16[1024,256]{1,0:T(8,128)(2,1)S(1)} %select_select_fusion.refs_2_), channel_id=1, source_target_pairs={{0,2},{1,3},{2,6},{3,7},{4,0},{5,1},{6,4},{7,5},{8,10},{9,11},{10,... | collective-permute-start | bytes 1572872 | tf_op jit(solution)/shard_map/ppermute | solution.py:247
  37.1 4.6 %collective-permute-start.7 = (bf16[1024,256]{1,0:T(8,128)(2,1)S(1)}, bf16[1024,256]{1,0:T(8,128)(2,1)S(1)}, u32[]{:S(2)}, u32[]{:S(2)}) collective-permute-start(bf16[1024,256]{1,0:T(8,128)(2,1)S(1)} %collective-permute-done.4.refs_4_), channel_id=1, source_target_pairs={{0,1},{1,0},{2,3},{3,2},{4,5},{5,4},{6,7},{7,6},{8,9},{9,8},{10,11... | collective-permute-start | bytes 1572872 | tf_op jit(solution)/shard_map/ppermute | solution.py:248
  37.1 15.2 %collective-permute-start.6 = (bf16[1024,256]{1,0:T(8,128)(2,1)S(1)}, bf16[1024,256]{1,0:T(8,128)(2,1)S(1)}, u32[]{:S(2)}, u32[]{:S(2)}) collective-permute-start(bf16[1024,256]{1,0:T(8,128)(2,1)S(1)} %collective-permute-done.4.refs_4_), channel_id=1, source_target_pairs={{0,2},{1,3},{2,6},{3,7},{4,0},{5,1},{6,4},{7,5},{8,10},{9,11},{10,... | collective-permute-start | bytes 1572872 | tf_op jit(solution)/shard_map/ppermute | solution.py:247
  52.3 23.4 %slice-start = ((s8[8388608]{0:T(1024)(128)(4,1)}), s8[4194304]{0:T(1024)(128)(4,1)S(1)}, s32[]{:S(2)}) async-start(s8[8388608]{0:T(1024)(128)(4,1)} %bitcast.33), calls=%async_computation | async-start | bytes 8388608
  52.3 23.4 %copy-start.4 = (bf16[1,128,2048]{2,1,0:T(8,128)(2,1)S(1)}, bf16[1,128,2048]{2,1,0:T(8,128)(2,1)}, u32[]{:S(2)}) copy-start(bf16[1,128,2048]{2,1,0:T(8,128)(2,1)} %param.14) | copy-start | bytes 1572868
  52.3 4.6 %collective-permute-start.9 = (bf16[1024,256]{1,0:T(8,128)(2,1)S(1)}, bf16[1024,256]{1,0:T(8,128)(2,1)S(1)}, u32[]{:S(2)}, u32[]{:S(2)}) collective-permute-start(bf16[1024,256]{1,0:T(8,128)(2,1)S(1)} %collective-permute-done.6.refs_4_), channel_id=1, source_target_pairs={{0,1},{1,0},{2,3},{3,2},{4,5},{5,4},{6,7},{7,6},{8,9},{9,8},{10,11... | collective-permute-start | bytes 1572872 | tf_op jit(solution)/shard_map/ppermute | solution.py:248
  52.3 15.2 %collective-permute-start.8 = (bf16[1024,256]{1,0:T(8,128)(2,1)S(1)}, bf16[1024,256]{1,0:T(8,128)(2,1)S(1)}, u32[]{:S(2)}, u32[]{:S(2)}) collective-permute-start(bf16[1024,256]{1,0:T(8,128)(2,1)S(1)} %collective-permute-done.6.refs_4_), channel_id=1, source_target_pairs={{0,2},{1,3},{2,6},{3,7},{4,0},{5,1},{6,4},{7,5},{8,10},{9,11},{10,... | collective-permute-start | bytes 1572872 | tf_op jit(solution)/shard_map/ppermute | solution.py:247
  67.6 3.7 %collective-permute-start.10 = (bf16[1024,256]{1,0:T(8,128)(2,1)S(1)}, bf16[1024,256]{1,0:T(8,128)(2,1)S(1)}, u32[]{:S(2)}, u32[]{:S(2)}) collective-permute-start(bf16[1024,256]{1,0:T(8,128)(2,1)S(1)} %collective-permute-done.8.refs_4_), channel_id=1, source_target_pairs={{0,1},{1,0},{2,3},{3,2},{4,5},{5,4},{6,7},{7,6},{8,9},{9,8},{10,11... | collective-permute-start | bytes 1572872 | tf_op jit(solution)/shard_map/ppermute | solution.py:248
  77.7 15.3 %collective-permute-start.11 = (bf16[128,2048]{1,0:T(8,128)(2,1)S(1)}, bf16[128,2048]{1,0:T(8,128)(2,1)S(1)}, u32[]{:S(2)}, u32[]{:S(2)}) collective-permute-start(bf16[128,2048]{1,0:T(8,128)(2,1)S(1)} %add_convert_fusion.2.rows_ref), channel_id=1, source_target_pairs={{0,2},{1,3},{2,6},{3,7},{4,0},{5,1},{6,4},{7,5},{8,10},{9,11},{10,... | collective-permute-start | bytes 1572872 | tf_op jit(solution)/shard_map/ppermute | solution.py:247
  93.0 15.7 %collective-permute-start.12 = (bf16[128,2048]{1,0:T(8,128)(2,1)S(1)}, bf16[128,2048]{1,0:T(8,128)(2,1)S(1)}, u32[]{:S(2)}, u32[]{:S(2)}) collective-permute-start(bf16[128,2048]{1,0:T(8,128)(2,1)S(1)} %collective-permute-done.11.rows_ref), channel_id=1, source_target_pairs={{0,2},{1,3},{2,6},{3,7},{4,0},{5,1},{6,4},{7,5},{8,10},{9,11},{10,... | collective-permute-start | bytes 1572872 | tf_op jit(solution)/shard_map/ppermute | solution.py:247
  96.8 23.1 %collective-permute-start.14 = (bf16[128,2048]{1,0:T(8,128)(2,1)S(1)}, bf16[128,2048]{1,0:T(8,128)(2,1)S(1)}, u32[]{:S(2)}, u32[]{:S(2)}) collective-permute-start(bf16[128,2048]{1,0:T(8,128)(2,1)S(1)} %convert_element_type.45), channel_id=1, source_target_pairs={{0,2},{1,3},{2,6},{3,7},{4,0},{5,1},{6,4},{7,5},{8,10},{9,11},{10,... | collective-permute-start | bytes 1572872 | tf_op jit(solution)/shard_map/ppermute | solution.py:247
  108.7 22.5 %collective-permute-start.13 = (bf16[128,2048]{1,0:T(8,128)(2,1)S(1)}, bf16[128,2048]{1,0:T(8,128)(2,1)S(1)}, u32[]{:S(2)}, u32[]{:S(2)}) collective-permute-start(bf16[128,2048]{1,0:T(8,128)(2,1)S(1)} %collective-permute-done.12.rows_ref), channel_id=1, source_target_pairs={{0,2},{1,3},{2,6},{3,7},{4,0},{5,1},{6,4},{7,5},{8,10},{9,11},{10,... | collective-permute-start | bytes 1572872 | tf_op jit(solution)/shard_map/ppermute | solution.py:247
  120.1 22.1 %copy-start.8 = (s32[1,8]{1,0:T(1,128)S(1)}, s32[1,8]{1,0:T(1,128)}, u32[]{:S(2)}) copy-start(s32[1,8]{1,0:T(1,128)} %param.16) | copy-start | bytes 100
  120.1 22.7 %copy-start.9 = (s32[1,8]{1,0:T(1,128)S(1)}, s32[1,8]{1,0:T(1,128)}, u32[]{:S(2)}) copy-start(s32[1,8]{1,0:T(1,128)} %param.15) | copy-start | bytes 100
  120.1 21.1 %collective-permute-start.15 = (bf16[128,2048]{1,0:T(8,128)(2,1)S(1)}, bf16[128,2048]{1,0:T(8,128)(2,1)S(1)}, u32[]{:S(2)}, u32[]{:S(2)}) collective-permute-start(bf16[128,2048]{1,0:T(8,128)(2,1)S(1)} %add_convert_fusion.1), channel_id=1, source_target_pairs={{0,2},{1,3},{2,6},{3,7},{4,0},{5,1},{6,4},{7,5},{8,10},{9,11},{10,... | collective-permute-start | bytes 1572872 | tf_op jit(solution)/shard_map/ppermute | solution.py:247
  141.3 13.6 %collective-permute-start.16 = (bf16[128,2048]{1,0:T(8,128)(2,1)S(1)}, bf16[128,2048]{1,0:T(8,128)(2,1)S(1)}, u32[]{:S(2)}, u32[]{:S(2)}) collective-permute-start(bf16[128,2048]{1,0:T(8,128)(2,1)S(1)} %add_convert_fusion), channel_id=1, source_target_pairs={{0,2},{1,3},{2,6},{3,7},{4,0},{5,1},{6,4},{7,5},{8,10},{9,11},{10,... | collective-permute-start | bytes 1572872 | tf_op jit(solution)/shard_map/ppermute | solution.py:247
  144.1 11.8 %copy-start.1 = (bf16[2048,256]{1,0:T(8,128)(2,1)S(1)}, bf16[2048,256]{1,0:T(8,128)(2,1)}, u32[]{:S(2)}) copy-start(bf16[2048,256]{1,0:T(8,128)(2,1)} %param.22) | copy-start | bytes 3145732
  (5 other events, 17.8 us)

commit v3 on v2

v3 whole, which is shorter than its diff:
```python
import functools
import math

import jax
import jax.numpy as jnp
from jax import lax
from jax.experimental import pallas as pl
from jax.experimental.pallas import tpu as pltpu
from jax.sharding import PartitionSpec as P

EPSILON = 1e-05
NEGATIVE = -1e30
HEADS_AT_ONCE = 8
HEADS_STACKED = 2
PARTS = 2


def layer_norm(values, gain, bias):
    average = jnp.mean(values, axis=-1, keepdims=True)
    centered = values - average
    spread = jnp.mean(centered * centered, axis=-1, keepdims=True)
    return centered * lax.rsqrt(spread + EPSILON) * gain + bias


def pick_value(table, wanted):
    slots_at = lax.broadcasted_iota(jnp.int32, table.shape, 0)
    return jnp.sum(jnp.where(slots_at == wanted, table, 0))


def ring_order(chips):
    return list(range(0, 1)) + list(range(1, chips, 2)) + list(range(chips - 2 + chips % 2, 0, -2))


def attend_kernel(first, last, head_size, group, carried, *refs):
    refs = list(refs)
    if carried:
        semaphores = refs.pop()
        targets, refs = refs[-carried:], refs[:-carried]
        outs = 1 if last else 3
        sources = refs[-outs - carried : -outs]
        del refs[-outs - carried : -outs]
        copies = [
            pltpu.make_async_copy(source, target, semaphores.at[i])
            for i, (source, target) in enumerate(zip(sources, targets))
        ]

        @pl.when(pl.program_id(0) == 0)
        def _():
            for copy in copies:
                copy.start()

    query_ref = refs.pop(0)
    if first:
        own_ref = refs.pop(0)
    else:
        weighted_in, highest_in, denominator_in = refs[:3]
        del refs[:3]
    outs = 1 if last else 3
    block_refs, out_refs = refs[:-outs], refs[-outs:]
    rows = query_ref.shape[0]
    heads = query_ref.shape[1] // head_size
    parts = [jnp.concatenate([ref[...] for ref in block_refs], axis=0)]
    if first:
        parts.insert(0, own_ref[...])

    def stacked(ref, start):
        return jnp.concatenate(
            [ref[:, (start + h) * head_size : (start + h + 1) * head_size] for h in range(group)], axis=0
        )

    def all_scores(start):
        queries = stacked(query_ref, start)
        result = []
        for part in parts:
            scores = lax.dot_general(
                queries, part[:, :head_size], (((1,), (1,)), ((), ())), preferred_element_type=jnp.float32
            )
            result.append(scores)
        if first:
            row_at = lax.broadcasted_iota(jnp.int32, result[0].shape, 0) % rows
            column_at = lax.broadcasted_iota(jnp.int32, result[0].shape, 1)
            result[0] = jnp.where(column_at <= row_at, result[0], NEGATIVE)
        return result

    def fold(start, scores):
        highest = None
        for part in scores:
            top = jnp.max(part, axis=-1, keepdims=True)
            highest = top if highest is None else jnp.maximum(highest, top)
        weighted, denominator = None, None
        if not first:
            before = jnp.concatenate([highest_in[start + h] for h in range(group)], axis=0)
            highest = jnp.maximum(highest, before)
            rescale = jnp.exp2(before - highest)
            weighted = stacked(weighted_in, start) * rescale
            denominator = (
                jnp.concatenate([denominator_in[start + h] for h in range(group)], axis=0) * rescale
            )
        for part, ref in zip(scores, parts):
            exponent = jnp.exp2(part - highest)
            total = jnp.sum(exponent, axis=-1, keepdims=True)
            product = jnp.dot(
                exponent.astype(jnp.bfloat16), ref[:, head_size:], preferred_element_type=jnp.float32
            )
            weighted = product if weighted is None else weighted + product
            denominator = total if denominator is None else denominator + total
        if last:
            weighted = weighted / denominator
        for h in range(group):
            at = start + h
            part = slice(h * rows, (h + 1) * rows)
            out_refs[0][:, at * head_size : (at + 1) * head_size] = weighted[part].astype(out_refs[0].dtype)
            if not last:
                out_refs[1][at] = highest[part]
                out_refs[2][at] = denominator[part]

    scores = all_scores(0)
    for start in range(0, heads, group):
        following = all_scores(start + group) if start + group < heads else None
        fold(start, scores)
        scores = following

    if carried:

        @pl.when(pl.program_id(0) == pl.num_programs(0) - 1)
        def _():
            for copy in copies:
                copy.wait()


def attend(queries, own, state, blocks, last, head_size, share=(0, 1), carried=()):
    rows, width = queries.shape[0] // share[1], queries.shape[1]
    heads = width // head_size
    at_once = math.gcd(heads, HEADS_AT_ONCE * share[1])
    wide = at_once * head_size
    first = state is None
    flat = pl.BlockSpec((rows, wide), lambda i: (share[0], i))
    stat = pl.BlockSpec((at_once, rows, 1), lambda i: (i, share[0], 0))
    whole = lambda array: pl.BlockSpec(array.shape, lambda i: (0, 0))
    in_specs = [flat] + ([whole(own)] if first else [flat, stat, stat]) + [whole(b) for b in blocks]
    operands = [queries] + ([own] if first else list(state)) + list(blocks)
    if last:
        out_specs = [pl.BlockSpec((rows, wide), lambda i: (0, i))]
        out_shape = [jax.ShapeDtypeStruct((rows, width), jnp.bfloat16)]
    else:
        out_specs = [flat, stat, stat]
        out_shape = [jax.ShapeDtypeStruct((rows, width), jnp.float32)] + [
            jax.ShapeDtypeStruct((heads, rows, 1), jnp.float32)
        ] * 2
    keys = sum(b.shape[0] for b in blocks) + (own.shape[0] if first else 0)
    outs = len(out_shape)
    result = pl.pallas_call(
        functools.partial(
            attend_kernel, first, last, head_size, math.gcd(at_once, HEADS_STACKED * share[1]), len(carried)
        ),
        grid=(heads // at_once,),
        in_specs=in_specs + [pl.BlockSpec(memory_space=pltpu.HBM)] * len(carried),
        out_specs=out_specs + [pl.BlockSpec(memory_space=pl.ANY)] * len(carried),
        out_shape=out_shape + [pltpu.VMEM(w.shape, w.dtype) for w in carried],
        scratch_shapes=[pltpu.SemaphoreType.DMA((len(carried),))] if carried else [],
        cost_estimate=pl.CostEstimate(
            flops=0 if last else 4 * rows * width * keys,
            bytes_accessed=0 if last else 2 * keys * 2 * head_size + 8 * rows * width,
            transcendentals=0 if last else rows * heads * keys,
        ),
        compiler_params=pltpu.CompilerParams(vmem_limit_bytes=20 * 1024 * 1024),
    )(*operands, *carried)
    return (result[0] if last else list(result[:outs])), list(result[outs:])


def hold_kernel(count, *refs):
    sources, held, done_ref, semaphores = refs[:count], refs[count:-2], refs[-2], refs[-1]
    copies = [
        pltpu.make_async_copy(sources[i], held[i], semaphores.at[i]) for i in range(count)
    ]
    for copy in copies:
        copy.start()
    done_ref[...] = jnp.zeros_like(done_ref)
    for copy in copies:
        copy.wait()


def hold(weights, room):
    count = len(weights)
    size = sum(w.size * w.dtype.itemsize for w in weights)
    return pl.pallas_call(
        functools.partial(hold_kernel, count),
        in_specs=[pl.BlockSpec(memory_space=pltpu.HBM)] * count,
        out_specs=[pl.BlockSpec(memory_space=pltpu.VMEM)] * (count + 1),
        out_shape=[pltpu.VMEM(w.shape, w.dtype) for w in weights] + [jax.ShapeDtypeStruct((8, 128), jnp.float32)],
        scratch_shapes=[pltpu.SemaphoreType.DMA((count,))],
        cost_estimate=pl.CostEstimate(flops=0, bytes_accessed=size, transcendentals=0),
        compiler_params=pltpu.CompilerParams(vmem_limit_bytes=room * 1024 * 1024),
    )(*weights)


def feed_forward_kernel(count, rows_ref, *refs):
    expands, contracts, out_ref = refs[:count], refs[count : 2 * count], refs[-1]
    out_ref[...] = jnp.zeros_like(out_ref)
    for expand_ref, contract_ref in zip(expands, contracts):
        extent = expand_ref.shape[1]
        stride = math.gcd(extent, 512)

        @pl.loop(0, extent // stride)
        def _(index):
            at = pl.ds(pl.multiple_of(index * stride, stride), stride)
            hidden = jnp.dot(rows_ref[...], expand_ref[:, at], preferred_element_type=jnp.float32)
            hidden = jax.nn.gelu(hidden, approximate=True).astype(jnp.bfloat16)
            out_ref[...] += jnp.dot(hidden, contract_ref[at, :], preferred_element_type=jnp.float32)


def feed_forward(rows, expands, contracts, held):
    return pl.pallas_call(
        functools.partial(feed_forward_kernel, len(expands)),
        in_specs=[pl.BlockSpec(memory_space=pltpu.VMEM)] * (1 + len(expands) + len(contracts) + len(held)),
        out_specs=pl.BlockSpec(memory_space=pltpu.VMEM),
        out_shape=jax.ShapeDtypeStruct(rows.shape, jnp.float32),
        cost_estimate=pl.CostEstimate(flops=0, bytes_accessed=0, transcendentals=0),
        compiler_params=pltpu.CompilerParams(vmem_limit_bytes=16 * 1024 * 1024),
    )(rows, *expands, *contracts, *held)


def finish_kernel(share, attended_ref, weight_ref, tokens_ref, gain_ref, bias_ref, residual_ref, second_ref):
    rows = attended_ref.shape[0]
    tokens = tokens_ref[share * rows : (share + 1) * rows].astype(jnp.float32)
    residual = tokens + jnp.dot(
        attended_ref[...], weight_ref[...], preferred_element_type=jnp.float32
    )
    residual_ref[...] = residual
    second_ref[...] = layer_norm(residual, gain_ref[...], bias_ref[...]).astype(jnp.bfloat16)


def finish(attended, weight, tokens, gain, bias, share):
    inside = pl.BlockSpec(memory_space=pltpu.VMEM)
    return pl.pallas_call(
        functools.partial(finish_kernel, share),
        in_specs=[inside] * 5,
        out_specs=[inside] * 2,
        out_shape=[
            jax.ShapeDtypeStruct(attended.shape, jnp.float32),
            jax.ShapeDtypeStruct(attended.shape, jnp.bfloat16),
        ],
        cost_estimate=pl.CostEstimate(flops=0, bytes_accessed=0, transcendentals=0),
        compiler_params=pltpu.CompilerParams(vmem_limit_bytes=16 * 1024 * 1024),
    )(attended, weight, tokens, gain[None], bias[None])


def first_hop(own, owners, sizes):
    groups, members = sizes
    group_index = lax.axis_index("group")
    member_index = lax.axis_index("member")
    wanted = pick_value(owners, group_index)
    if groups != 4:
        every_block = lax.all_gather(own, "group", axis=0)
        chosen = lax.dynamic_index_in_dim(every_block, wanted, 0, keepdims=False)
        return chosen, lambda chosen: chosen
    near = 1 + member_index % 2
    far = 3 - near

    def step(block, flip):
        pairs = [
            (g * members + m, (g ^ (flip ^ (3 * (m % 2)))) * members + m)
            for g in range(groups)
            for m in range(members)
        ]
        return lax.ppermute(block, ("group", "member"), pairs)

    wanted_there = pick_value(owners, group_index ^ far)

    def second_hop(beside):
        passed = jnp.where(wanted_there == (group_index ^ near), beside, own)
        across = step(passed, 2)
        return jnp.where(
            wanted == group_index, own, jnp.where(wanted == (group_index ^ near), beside, across)
        )

    return step(own, 1), second_hop


def project_kernel(
    factor, tokens_ref, gain_ref, bias_ref, query_ref, keyval_ref, queries_ref, keys_values_ref, held, semaphores
):
    count, _, stride = held.shape
    copies = [
        pltpu.make_async_copy(
            query_ref.at[:, pl.ds(i * stride, stride)], held.at[i], semaphores.at[i]
        )
        for i in range(count)
    ]
    for copy in copies:
        copy.start()
    values = tokens_ref[...].astype(jnp.float32)
    normed = layer_norm(values, gain_ref[...], bias_ref[...]).astype(jnp.bfloat16)
    keys_values_ref[...] = jnp.dot(
        normed, keyval_ref[...], preferred_element_type=jnp.float32
    ).astype(jnp.bfloat16)
    for i, copy in enumerate(copies):
        copy.wait()
        queries = jnp.dot(normed, held[i], preferred_element_type=jnp.float32)
        queries_ref[:, i * stride : (i + 1) * stride] = (queries * factor).astype(jnp.bfloat16)


def project(tokens, gain, bias, query_weight, keyval_weight, factor):
    rows, width = tokens.shape
    wide, narrow = query_weight.shape[1], keyval_weight.shape[1]
    stride = math.gcd(wide, 512)
    inside = pl.BlockSpec(memory_space=pltpu.VMEM)
    return pl.pallas_call(
        functools.partial(project_kernel, factor),
        in_specs=[inside, inside, inside, pl.BlockSpec(memory_space=pltpu.HBM), inside],
        out_specs=[inside, inside],
        out_shape=[
            jax.ShapeDtypeStruct((rows, wide), jnp.bfloat16),
            jax.ShapeDtypeStruct((rows, narrow), jnp.bfloat16),
        ],
        scratch_shapes=[
            pltpu.VMEM((wide // stride, width, stride), jnp.bfloat16),
            pltpu.SemaphoreType.DMA((wide // stride,)),
        ],
        cost_estimate=pl.CostEstimate(
            flops=2 * rows * width * (wide + narrow),
            bytes_accessed=2 * width * (wide + narrow),
            transcendentals=rows,
        ),
        compiler_params=pltpu.CompilerParams(vmem_limit_bytes=58 * 1024 * 1024),
    )(tokens, gain[None], bias[None], query_weight, keyval_weight)


def shards(
    sizes,
    activations,
    lengths,
    assignment,
    owners,
    prefix_cache,
    first_gain,
    first_bias,
    query_weight,
    keyval_weight,
    output_weight,
    second_gain,
    second_bias,
    expand_weight,
    contract_weight,
):
    groups, members = sizes
    chips = members // 2
    order = ring_order(chips)
    after = {order[i]: order[(i + 1) % chips] for i in range(chips)}
    ring_pairs = [(2 * z + c, 2 * after[z] + c) for z in range(chips) for c in range(2)]
    swap_pairs = [(m, m ^ 1) for m in range(members)]
    ring = lambda block: lax.ppermute(block, "member", ring_pairs)
    swap = lambda block: lax.ppermute(block, "member", swap_pairs)

    tokens = activations[0]
    row_count = tokens.shape[0]
    head_size = prefix_cache.shape[2] // 2

    beside, second_hop = first_hop(prefix_cache[0], owners, sizes)
    expand_other = swap(expand_weight)
    contract_other = swap(contract_weight)

    factor = math.log2(math.e) / math.sqrt(head_size)
    queries, keys_values = project(
        tokens, first_gain, first_bias, query_weight, keyval_weight, factor
    )
    beside, queries, keys_values, expand_other = lax.optimization_barrier(
        (beside, queries, keys_values, expand_other)
    )
    block = second_hop(beside)
    expand_here, contract_here, held_here = hold((expand_weight, contract_weight), 50)
    block, held_here, contract_other = lax.optimization_barrier((block, held_here, contract_other))

    count = chips * PARTS
    pieces = list(jnp.split(block, PARTS))
    pieces += [ring(piece) for piece in pieces] if chips > 1 else []
    work = [pieces[:PARTS], [swap(block)]]
    state, carried, held = None, [expand_other, contract_other], []
    for i in range(PARTS, count):
        state, brought = attend(
            queries, keys_values, state, work.pop(0), False, head_size, carried=carried[:1]
        )
        carried, held = carried[1:], held + brought
        pieces[i], state = lax.optimization_barrier((pieces[i], state))
        if i + PARTS < count:
            pieces.append(ring(pieces[i]))
        work.append([pieces[i], swap(pieces[i])])
    while len(work) > 1:
        state, brought = attend(
            queries, keys_values, state, work.pop(0), False, head_size, carried=carried[:1]
        )
        carried, held = carried[1:], held + brought
    expand_other, contract_other = held

    blocks, residual, rows = work[0], [], []
    for i in range(PARTS):
        attended, _ = attend(queries, keys_values, state, blocks, True, head_size, (i, PARTS))
        ahead, behind = finish(attended, output_weight, tokens, second_gain, second_bias, i)
        residual.append(ahead)
        rows.append(behind)
        blocks[0], rows[i] = lax.optimization_barrier((blocks[0], rows[i]))

    expands, contracts = (expand_here, expand_other), (contract_here, contract_other)
    held = [held_here]
    second = jnp.concatenate(rows, axis=0)
    arriving = [ring(part) for part in rows]
    before, summed = None, [None] * PARTS
    for step in range(1, chips):
        for i in range(PARTS):
            if before is None:
                rows[i] = arriving[i]
            else:
                rows[i], before = lax.optimization_barrier((arriving[i], before))
            if step < chips - 1:
                arriving[i] = ring(rows[i])
            part = feed_forward(rows[i], expands, contracts, held)
            before = part
            part = part if step == 1 else part + summed[i].astype(jnp.float32)
            summed[i] = ring(part.astype(jnp.bfloat16))
    second, before, lengths, assignment = lax.optimization_barrier(
        (second, before, lengths, assignment)
    )
    here = feed_forward(second, expands, contracts, held)
    total = jnp.concatenate(residual, axis=0) + here + jnp.concatenate(summed, axis=0).astype(jnp.float32)
    member_index = lax.axis_index("member")
    request = pick_value(assignment[0], member_index)
    length_here = pick_value(lengths[0], request)
    is_live = lax.broadcasted_iota(jnp.int32, (row_count, 1), 0) < length_here
    return jnp.where(is_live, total, 0.0).astype(jnp.bfloat16)[None]


def solution(mesh):
    sizes = (mesh.shape["group"], mesh.shape["member"])
    return jax.shard_map(
        functools.partial(shards, sizes),
        mesh=mesh,
        in_specs=(
            P("group", "member", None),
            P("group", None),
            P("group", None),
            P(),
            P("group", "member", None),
            P(),
            P(),
            P(),
            P(),
            P(),
            P(),
            P(),
            P(None, "member"),
            P("member", None),
        ),
        out_specs=P("group", "member", None),
        check_vma=False,
    )
```

time: 156 us -> 140 us (0.90)
  waiting for transfers between devices: 72.2 us -> 24.4 us
  Pallas kernels: 46 us -> 71 us
  starting transfers between devices: 17.4 us -> 36.3 us
  matrix products: 7.75 us -> 0 us
  other arithmetic: 9.6 us -> 5.4 us
    ppermute x9 -> x18, waiting for transfers between devices: 69.7 us -> 22 us  [shards(): ring = lambda block: lax.ppermute(block, 'member', ring_pairs)]
    ppermute x9 -> x18, starting transfers between devices: 11.8 us -> 30.9 us  [shards(): ring = lambda block: lax.ppermute(block, 'member', ring_pairs)]
    pallas_call x4 -> x7, Pallas kernels: 11.8 us -> 26.8 us  [feed_forward(): pl.pallas_call(functools.partial(feed_forward_kernel, len(expands)), in_s...]
    pallas_call x0 -> x3, Pallas kernels: none -> 9.9 us  [the longest x1 6.27 us: project(): pl.pallas_call(functools.partial(project_kernel, factor), in_specs=[insid...]
    dot_general x3 -> x0, matrix products: 7.75 us -> none  [the longest x1 4.95 us: shards(): queries = jnp.dot(normed, query_weight, preferred_element_type=jnp.float32)]
    reduce_sum x3 -> x0, other arithmetic: 2.78 us -> none  [the longest x2 1.59 us: layer_norm(): spread = jnp.mean(centered * centered, axis=-1, keepdims=True)]
    pallas_call x2 -> x1, Pallas kernels: 4.06 us -> 4.12 us  [hold(): pl.pallas_call(functools.partial(hold_kernel, count), in_specs=[pl.BlockS...]
    pallas_call x8 -> x9, Pallas kernels: 30.2 us -> 30.2 us  [attend(): pl.pallas_call(functools.partial(attend_kernel, first, last, head_size, m...]
  transfers between devices with their start and end apart: 17 -> 29, of which waited for: 11 -> 12; matrix products, arithmetic and copies ran while one was open for 9% -> 3% of each run, Pallas kernels for 27% -> 48%
where the time goes in v3:
time: 140 us; the launch traced here: 139 us
  Pallas kernels  71 us (51%)
  starting transfers between devices  36.3 us (26%)
  waiting for transfers between devices  24.4 us (17%)
  other arithmetic  5.4 us (4%)
  between operations  2.22 us (2%)
    ppermute x18, starting transfers between devices, shards(): ring = lambda block: lax.ppermute(block, 'member', ring_pairs)  30.9 us
    pallas_call x9, Pallas kernels, attend(): pl.pallas_call(functools.partial(attend_kernel, first, last, head_size, m...  30.2 us
    pallas_call x7, Pallas kernels, feed_forward(): pl.pallas_call(functools.partial(feed_forward_kernel, len(expands)), in_s...  26.8 us
    ppermute x18, waiting for transfers between devices, shards(): ring = lambda block: lax.ppermute(block, 'member', ring_pairs)  22 us
    pallas_call x1, Pallas kernels, project(): pl.pallas_call(functools.partial(project_kernel, factor), in_specs=[insid...  6.27 us
    ppermute x2, starting transfers between devices, step(): return lax.ppermute(block, ('group', 'member'), pairs)  4.52 us
    pallas_call x1, Pallas kernels, hold(): pl.pallas_call(functools.partial(hold_kernel, count), in_specs=[pl.BlockS...  4.12 us
    pallas_call x2, Pallas kernels, finish(): pl.pallas_call(functools.partial(finish_kernel, share), in_specs=[inside]...  3.64 us
  transfers between devices with their start and end apart: 29, of which 12 were waited for; matrix products, arithmetic and copies ran while one was open for 3% of the time, Pallas kernels for 48%

profile of v3, /device:TPU:0, one launch (start us, length us, event | category | flops | bytes accessed | tf_op | source)
XLA Modules:
  0.0 139.3 jit_solution(2930017213899089666)
XLA Ops:
  0.5 2.9 %collective-permute-start = (bf16[1024,256]{1,0:T(8,128)(2,1)}, bf16[1024,256]{1,0:T(8,128)(2,1)S(1)}, u32[]{:S(2)}, u32[]{:S(2)}) collective-permute-start(bf16[1024,256]{1,0:T(8,128)(2,1)} %bitcast.23), channel_id=1, source_target_pairs={{0,8},{1,17},{2,10},{3,19},{4,12},{5,21},{6,14},{7,23},{8,0},{9,25... | collective-permute-start | bytes 1572872 | tf_op jit(solution)/shard_map/ppermute | solution.py:266
  5.4 6.3 %shard_map.136 = (bf16[128,2048]{1,0:T(8,128)(2,1)}, bf16[128,256]{1,0:T(8,128)(2,1)}) custom-call(bf16[128,2048]{1,0:T(8,128)(2,1)} %bitcast.16, f32[1,2048]{1,0:T(1,128)} %bitcast.24, f32[1,2048]{1,0:T(1,128)} %bitcast.25, bf16[2048,2048]{1,0:T(8,128)(2,1)} %query_ref.1, bf16[2048,256]{1,0:T(8,128)(2,1)} %keyval_ref.1), custom_call_target="tpu_custom_call" | custom-call | flops 1207959552 | bytes 9437184 | tf_op jit(solution)/shard_map/pallas_call | solution.py:308
  14.5 4.1 %shard_map.137 = (bf16[2048,1024]{1,0:T(8,128)(2,1)S(1)}, bf16[1024,2048]{1,0:T(8,128)(2,1)S(1)}, f32[8,128]{1,0:T(8,128)}) custom-call(bf16[2048,1024]{1,0:T(8,128)(2,1)} %refs_0_.1, bf16[1024,2048]{1,0:T(8,128)(2,1)} %refs_1_.1), custom_call_target="tpu_custom_call" | custom-call | bytes 8388608 | tf_op jit(solution)/shard_map/pallas_call | solution.py:186
  22.9 2.6 %collective-permute-start.4 = (bf16[512,256]{1,0:T(8,128)(2,1)S(1)}, bf16[512,256]{1,0:T(8,128)(2,1)S(1)}, u32[]{:S(2)}, u32[]{:S(2)}) collective-permute-start(bf16[512,256]{1,0:T(8,128)(2,1)S(1)} %get-tuple-element.156.refs_3_), channel_id=1, source_target_pairs={{0,2},{1,3},{2,6},{3,7},{4,0},{5,1},{6,4},{7,5},{8,10},{9,11},{10,... | collective-permute-start | bytes 786440 | tf_op jit(solution)/shard_map/ppermute | solution.py:352
  25.5 3.7 %shard_map.138 = (f32[128,2048]{1,0:T(8,128)S(1)}, f32[16,128,1]{2,1,0:T(8,128)S(1)}, f32[16,128,1]{2,1,0:T(8,128)S(1)}, bf16[2048,1024]{1,0:T(8,128)(2,1)S(1)}) custom-call(bf16[128,2048]{1,0:T(8,128)(2,1)S(1)} %copy-done, bf16[128,256]{1,0:T(8,128)(2,1)S(1)} %copy-done.3, bf16[512,256]{1,0:T(8,128)(2,1)S(1)} %get-tuple-element.155.refs_2_, ...), custom_call_target="tpu_custom_call" | custom-call | flops 1207959552 | bytes 2686976 | tf_op jit(solution)/shard_map/pallas_call | solution.py:152
  32.1 3.8 %shard_map.139 = (f32[128,2048]{1,0:T(8,128)S(1)}, f32[16,128,1]{2,1,0:T(8,128)S(1)}, f32[16,128,1]{2,1,0:T(8,128)S(1)}, bf16[1024,2048]{1,0:T(8,128)(2,1)S(1)}) custom-call(bf16[128,2048]{1,0:T(8,128)(2,1)S(1)} %copy-done, f32[128,2048]{1,0:T(8,128)S(1)} %get-tuple-element.90.refs_1_, f32[16,128,1]{2,1,0:T(8,128)S(1)} %get-tuple-element.91.refs_2_, ...), custom_call_target="tpu_custom_call" | custom-call | flops 1073741824 | bytes 2621440 | tf_op jit(solution)/shard_map/pallas_call | solution.py:152
  36.9 2.6 %collective-permute-start.7 = (bf16[512,256]{1,0:T(8,128)(2,1)S(1)}, bf16[512,256]{1,0:T(8,128)(2,1)S(1)}, u32[]{:S(2)}, u32[]{:S(2)}) collective-permute-start(bf16[512,256]{1,0:T(8,128)(2,1)S(1)} %collective-permute-done.4.refs_4_), channel_id=1, source_target_pairs={{0,2},{1,3},{2,6},{3,7},{4,0},{5,1},{6,4},{7,5},{8,10},{9,11},{10,... | collective-permute-start | bytes 786440 | tf_op jit(solution)/shard_map/ppermute | solution.py:352
  39.6 3.7 %shard_map.140 = (f32[128,2048]{1,0:T(8,128)S(1)}, f32[16,128,1]{2,1,0:T(8,128)S(1)}, f32[16,128,1]{2,1,0:T(8,128)S(1)}) custom-call(bf16[128,2048]{1,0:T(8,128)(2,1)S(1)} %copy-done, f32[128,2048]{1,0:T(8,128)S(1)} %get-tuple-element.99.refs_1_, f32[16,128,1]{2,1,0:T(8,128)S(1)} %get-tuple-element.100.refs_2_, ...), custom_call_target="tpu_custom_call" | custom-call | flops 1073741824 | bytes 2621440 | tf_op jit(solution)/shard_map/pallas_call | solution.py:152
  45.1 3.7 %shard_map.141 = (f32[128,2048]{1,0:T(8,128)S(1)}, f32[16,128,1]{2,1,0:T(8,128)S(1)}, f32[16,128,1]{2,1,0:T(8,128)S(1)}) custom-call(bf16[128,2048]{1,0:T(8,128)(2,1)S(1)} %copy-done, f32[128,2048]{1,0:T(8,128)S(1)} %get-tuple-element.105.refs_1_, f32[16,128,1]{2,1,0:T(8,128)S(1)} %get-tuple-element.106.refs_2_, ...), custom_call_target="tpu_custom_call" | custom-call | flops 1073741824 | bytes 2621440 | tf_op jit(solution)/shard_map/pallas_call | solution.py:152
  50.8 3.7 %shard_map.142 = (f32[128,2048]{1,0:T(8,128)S(1)}, f32[16,128,1]{2,1,0:T(8,128)S(1)}, f32[16,128,1]{2,1,0:T(8,128)S(1)}) custom-call(bf16[128,2048]{1,0:T(8,128)(2,1)S(1)} %copy-done, f32[128,2048]{1,0:T(8,128)S(1)} %get-tuple-element.113.refs_1_, f32[16,128,1]{2,1,0:T(8,128)S(1)} %get-tuple-element.114.refs_2_, ...), custom_call_target="tpu_custom_call" | custom-call | flops 1073741824 | bytes 2621440 | tf_op jit(solution)/shard_map/pallas_call | solution.py:152
  54.6 3.7 %shard_map.143 = (f32[128,2048]{1,0:T(8,128)S(1)}, f32[16,128,1]{2,1,0:T(8,128)S(1)}, f32[16,128,1]{2,1,0:T(8,128)S(1)}) custom-call(bf16[128,2048]{1,0:T(8,128)(2,1)S(1)} %copy-done, f32[128,2048]{1,0:T(8,128)S(1)} %get-tuple-element.119.refs_1_, f32[16,128,1]{2,1,0:T(8,128)S(1)} %get-tuple-element.120.refs_2_, ...), custom_call_target="tpu_custom_call" | custom-call | flops 1073741824 | bytes 2621440 | tf_op jit(solution)/shard_map/pallas_call | solution.py:152
  59.1 3.7 %shard_map.144 = (f32[128,2048]{1,0:T(8,128)S(1)}, f32[16,128,1]{2,1,0:T(8,128)S(1)}, f32[16,128,1]{2,1,0:T(8,128)S(1)}) custom-call(bf16[128,2048]{1,0:T(8,128)(2,1)S(1)} %copy-done, f32[128,2048]{1,0:T(8,128)S(1)} %get-tuple-element.126.refs_1_, f32[16,128,1]{2,1,0:T(8,128)S(1)} %get-tuple-element.127.refs_2_, ...), custom_call_target="tpu_custom_call" | custom-call | flops 1073741824 | bytes 2621440 | tf_op jit(solution)/shard_map/pallas_call | solution.py:152
  72.3 2.8 %collective-permute-start.17 = (bf16[64,2048]{1,0:T(8,128)(2,1)S(1)}, bf16[64,2048]{1,0:T(8,128)(2,1)S(1)}, u32[]{:S(2)}, u32[]{:S(2)}) collective-permute-start(bf16[64,2048]{1,0:T(8,128)(2,1)S(1)} %get-tuple-element.137), channel_id=1, source_target_pairs={{0,2},{1,3},{2,6},{3,7},{4,0},{5,1},{6,4},{7,5},{8,10},{9,11},{10,... | collective-permute-start | bytes 786440 | tf_op jit(solution)/shard_map/ppermute | solution.py:352
  77.7 3.8 %shard_map.149 = f32[64,2048]{1,0:T(8,128)S(1)} custom-call(bf16[64,2048]{1,0:T(8,128)(2,1)S(1)} %collective-permute-done.18.rows_ref, bf16[2048,1024]{1,0:T(8,128)(2,1)S(1)} %get-tuple-element.138.refs_0_, bf16[2048,1024]{1,0:T(8,128)(2,1)S(1)} %get-tuple-element.139.refs_1_, bf16[1024,2048]{1,0:T(8,128)(2,1)S(1)} %get-tuple-element.140.refs_2_, ...), custom_call_target="tpu_custom_call" | custom-call | tf_op jit(solution)/shard_map/pallas_call | solution.py:213
  86.8 3.8 %shard_map.150 = f32[64,2048]{1,0:T(8,128)S(1)} custom-call(bf16[64,2048]{1,0:T(8,128)(2,1)S(1)} %collective-permute-done.17.rows_ref, bf16[2048,1024]{1,0:T(8,128)(2,1)S(1)} %get-tuple-element.138.refs_0_, bf16[2048,1024]{1,0:T(8,128)(2,1)S(1)} %get-tuple-element.139.refs_1_, bf16[1024,2048]{1,0:T(8,128)(2,1)S(1)} %get-tuple-element.140.refs_2_, ...), custom_call_target="tpu_custom_call" | custom-call | tf_op jit(solution)/shard_map/pallas_call | solution.py:213
  91.5 3.8 %shard_map.151 = f32[64,2048]{1,0:T(8,128)S(1)} custom-call(bf16[64,2048]{1,0:T(8,128)(2,1)S(1)} %collective-permute-done.20.rows_ref, bf16[2048,1024]{1,0:T(8,128)(2,1)S(1)} %get-tuple-element.138.refs_0_, bf16[2048,1024]{1,0:T(8,128)(2,1)S(1)} %get-tuple-element.139.refs_1_, bf16[1024,2048]{1,0:T(8,128)(2,1)S(1)} %get-tuple-element.140.refs_2_, ...), custom_call_target="tpu_custom_call" | custom-call | tf_op jit(solution)/shard_map/pallas_call | solution.py:213
  95.4 2.5 %collective-permute-start.21 = (bf16[64,2048]{1,0:T(8,128)(2,1)S(1)}, bf16[64,2048]{1,0:T(8,128)(2,1)S(1)}, u32[]{:S(2)}, u32[]{:S(2)}) collective-permute-start(bf16[64,2048]{1,0:T(8,128)(2,1)S(1)} %collective-permute-done.19.rows_ref), channel_id=1, source_target_pairs={{0,2},{1,3},{2,6},{3,7},{4,0},{5,1},{6,4},{7,5},{8,10},{9,11},{10,... | collective-permute-start | bytes 786440 | tf_op jit(solution)/shard_map/ppermute | solution.py:352
  97.9 3.8 %shard_map.152 = f32[64,2048]{1,0:T(8,128)S(1)} custom-call(bf16[64,2048]{1,0:T(8,128)(2,1)S(1)} %collective-permute-done.19.rows_ref, bf16[2048,1024]{1,0:T(8,128)(2,1)S(1)} %get-tuple-element.138.refs_0_, bf16[2048,1024]{1,0:T(8,128)(2,1)S(1)} %get-tuple-element.139.refs_1_, bf16[1024,2048]{1,0:T(8,128)(2,1)S(1)} %get-tuple-element.140.refs_2_, ...), custom_call_target="tpu_custom_call" | custom-call | tf_op jit(solution)/shard_map/pallas_call | solution.py:213
  106.8 3.8 %collective-permute-done.22.rows_ref = bf16[64,2048]{1,0:T(8,128)(2,1)S(1)} collective-permute-done((bf16[64,2048]{1,0:T(8,128)(2,1)S(1)}, bf16[64,2048]{1,0:T(8,128)(2,1)S(1)}, u32[]{:S(2)}, u32[]{:S(2)}) %collective-permute-start.22) | collective-permute-done | bytes 262176 | tf_op jit(solution)/shard_map/ppermute | solution.py:352
  110.6 3.8 %shard_map.153 = f32[64,2048]{1,0:T(8,128)S(1)} custom-call(bf16[64,2048]{1,0:T(8,128)(2,1)S(1)} %collective-permute-done.22.rows_ref, bf16[2048,1024]{1,0:T(8,128)(2,1)S(1)} %get-tuple-element.138.refs_0_, bf16[2048,1024]{1,0:T(8,128)(2,1)S(1)} %get-tuple-element.139.refs_1_, bf16[1024,2048]{1,0:T(8,128)(2,1)S(1)} %get-tuple-element.140.refs_2_, ...), custom_call_target="tpu_custom_call" | custom-call | tf_op jit(solution)/shard_map/pallas_call | solution.py:213
  116.2 3.8 %shard_map.154 = f32[64,2048]{1,0:T(8,128)S(1)} custom-call(bf16[64,2048]{1,0:T(8,128)(2,1)S(1)} %collective-permute-done.21.rows_ref, bf16[2048,1024]{1,0:T(8,128)(2,1)S(1)} %get-tuple-element.138.refs_0_, bf16[2048,1024]{1,0:T(8,128)(2,1)S(1)} %get-tuple-element.139.refs_1_, bf16[1024,2048]{1,0:T(8,128)(2,1)S(1)} %get-tuple-element.140.refs_2_, ...), custom_call_target="tpu_custom_call" | custom-call | tf_op jit(solution)/shard_map/pallas_call | solution.py:213
  123.7 3.8 %collective-permute-done.27 = bf16[64,2048]{1,0:T(8,128)(2,1)S(1)} collective-permute-done((bf16[64,2048]{1,0:T(8,128)(2,1)S(1)}, bf16[64,2048]{1,0:T(8,128)(2,1)S(1)}, u32[]{:S(2)}, u32[]{:S(2)}) %collective-permute-start.27) | collective-permute-done | bytes 262176 | tf_op jit(solution)/shard_map/ppermute | solution.py:352
  129.9 3.7 %shard_map.155 = f32[128,2048]{1,0:T(8,128)S(1)} custom-call(bf16[128,2048]{1,0:T(8,128)(2,1)S(1)} %pad_maximum_fusion.rows_ref, bf16[2048,1024]{1,0:T(8,128)(2,1)S(1)} %get-tuple-element.138.refs_0_, bf16[2048,1024]{1,0:T(8,128)(2,1)S(1)} %get-tuple-element.139.refs_1_, bf16[1024,2048]{1,0:T(8,128)(2,1)S(1)} %get-tuple-element.140.refs_2_, ...), custom_call_target="tpu_custom_call" | custom-call | tf_op jit(solution)/shard_map/pallas_call | solution.py:213
  135.6 2.7 %collective-permute-done.28 = bf16[64,2048]{1,0:T(8,128)(2,1)S(1)} collective-permute-done((bf16[64,2048]{1,0:T(8,128)(2,1)S(1)}, bf16[64,2048]{1,0:T(8,128)(2,1)S(1)}, u32[]{:S(2)}, u32[]{:S(2)}) %collective-permute-start.28) | collective-permute-done | bytes 262176 | tf_op jit(solution)/shard_map/ppermute | solution.py:352
  (92 shorter events, 50.3 us)
Async XLA Ops:
  0.0 11.7 %collective-permute-start.1 = (bf16[2048,1024]{1,0:T(8,128)(2,1)}, bf16[2048,1024]{1,0:T(8,128)(2,1)}, u32[]{:S(2)}, u32[]{:S(2)}) collective-permute-start(bf16[2048,1024]{1,0:T(8,128)(2,1)} %refs_0_.1), channel_id=1, source_target_pairs={{0,1},{1,0},{2,3},{3,2},{4,5},{5,4},{6,7},{7,6},{8,9},{9,8},{10,11... | collective-permute-start | bytes 12582920 | tf_op jit(solution)/shard_map/ppermute | solution.py:353
  0.5 20.7 %collective-permute-start.3 = (bf16[1024,2048]{1,0:T(8,128)(2,1)}, bf16[1024,2048]{1,0:T(8,128)(2,1)}, u32[]{:S(2)}, u32[]{:S(2)}) collective-permute-start(bf16[1024,2048]{1,0:T(8,128)(2,1)} %refs_1_.1), channel_id=1, source_target_pairs={{0,1},{1,0},{2,3},{3,2},{4,5},{5,4},{6,7},{7,6},{8,9},{9,8},{10,11... | collective-permute-start | bytes 12582920 | tf_op jit(solution)/shard_map/ppermute | solution.py:353
  0.5 11.2 %collective-permute-start = (bf16[1024,256]{1,0:T(8,128)(2,1)}, bf16[1024,256]{1,0:T(8,128)(2,1)S(1)}, u32[]{:S(2)}, u32[]{:S(2)}) collective-permute-start(bf16[1024,256]{1,0:T(8,128)(2,1)} %bitcast.23), channel_id=1, source_target_pairs={{0,8},{1,17},{2,10},{3,19},{4,12},{5,21},{6,14},{7,23},{8,0},{9,25... | collective-permute-start | bytes 1572872 | tf_op jit(solution)/shard_map/ppermute | solution.py:266
  11.8 9.2 %collective-permute-start.2 = (bf16[1024,256]{1,0:T(8,128)(2,1)S(1)}, bf16[1024,256]{1,0:T(8,128)(2,1)S(1)}, u32[]{:S(2)}, u32[]{:S(2)}) collective-permute-start(bf16[1024,256]{1,0:T(8,128)(2,1)S(1)} %broadcast_select_fusion), channel_id=1, source_target_pairs={{0,16},{1,9},{2,18},{3,11},{4,20},{5,13},{6,22},{7,15},{8,24},{9,1... | collective-permute-start | bytes 1572872 | tf_op jit(solution)/shard_map/ppermute | solution.py:266
  21.1 11.0 %collective-permute-start.6 = (bf16[1024,256]{1,0:T(8,128)(2,1)S(1)}, bf16[1024,256]{1,0:T(8,128)(2,1)S(1)}, u32[]{:S(2)}, u32[]{:S(2)}) collective-permute-start(bf16[1024,256]{1,0:T(8,128)(2,1)S(1)} %select_select_fusion), channel_id=1, source_target_pairs={{0,1},{1,0},{2,3},{3,2},{4,5},{5,4},{6,7},{7,6},{8,9},{9,8},{10,11... | collective-permute-start | bytes 1572872 | tf_op jit(solution)/shard_map/ppermute | solution.py:353
  21.2 10.1 %collective-permute-start.5 = (bf16[512,256]{1,0:T(8,128)(2,1)S(1)}, bf16[512,256]{1,0:T(8,128)(2,1)S(1)}, u32[]{:S(2)}, u32[]{:S(2)}) collective-permute-start(bf16[512,256]{1,0:T(8,128)(2,1)S(1)} %get-tuple-element.155.refs_2_), channel_id=1, source_target_pairs={{0,2},{1,3},{2,6},{3,7},{4,0},{5,1},{6,4},{7,5},{8,10},{9,11},{10,... | collective-permute-start | bytes 786440 | tf_op jit(solution)/shard_map/ppermute | solution.py:352
  22.9 14.0 %collective-permute-start.4 = (bf16[512,256]{1,0:T(8,128)(2,1)S(1)}, bf16[512,256]{1,0:T(8,128)(2,1)S(1)}, u32[]{:S(2)}, u32[]{:S(2)}) collective-permute-start(bf16[512,256]{1,0:T(8,128)(2,1)S(1)} %get-tuple-element.156.refs_3_), channel_id=1, source_target_pairs={{0,2},{1,3},{2,6},{3,7},{4,0},{5,1},{6,4},{7,5},{8,10},{9,11},{10,... | collective-permute-start | bytes 786440 | tf_op jit(solution)/shard_map/ppermute | solution.py:352
  31.3 8.3 %collective-permute-start.9 = (bf16[512,256]{1,0:T(8,128)(2,1)S(1)}, bf16[512,256]{1,0:T(8,128)(2,1)S(1)}, u32[]{:S(2)}, u32[]{:S(2)}) collective-permute-start(bf16[512,256]{1,0:T(8,128)(2,1)S(1)} %collective-permute-done.5.refs_4_), channel_id=1, source_target_pairs={{0,1},{1,0},{2,3},{3,2},{4,5},{5,4},{6,7},{7,6},{8,9},{9,8},{10,11... | collective-permute-start | bytes 786440 | tf_op jit(solution)/shard_map/ppermute | solution.py:353
  31.3 12.0 %collective-permute-start.8 = (bf16[512,256]{1,0:T(8,128)(2,1)S(1)}, bf16[512,256]{1,0:T(8,128)(2,1)S(1)}, u32[]{:S(2)}, u32[]{:S(2)}) collective-permute-start(bf16[512,256]{1,0:T(8,128)(2,1)S(1)} %collective-permute-done.5.refs_4_), channel_id=1, source_target_pairs={{0,2},{1,3},{2,6},{3,7},{4,0},{5,1},{6,4},{7,5},{8,10},{9,11},{10,... | collective-permute-start | bytes 786440 | tf_op jit(solution)/shard_map/ppermute | solution.py:352
  36.9 11.9 %collective-permute-start.7 = (bf16[512,256]{1,0:T(8,128)(2,1)S(1)}, bf16[512,256]{1,0:T(8,128)(2,1)S(1)}, u32[]{:S(2)}, u32[]{:S(2)}) collective-permute-start(bf16[512,256]{1,0:T(8,128)(2,1)S(1)} %collective-permute-done.4.refs_4_), channel_id=1, source_target_pairs={{0,2},{1,3},{2,6},{3,7},{4,0},{5,1},{6,4},{7,5},{8,10},{9,11},{10,... | collective-permute-start | bytes 786440 | tf_op jit(solution)/shard_map/ppermute | solution.py:352
  43.4 11.1 %collective-permute-start.12 = (bf16[512,256]{1,0:T(8,128)(2,1)S(1)}, bf16[512,256]{1,0:T(8,128)(2,1)S(1)}, u32[]{:S(2)}, u32[]{:S(2)}) collective-permute-start(bf16[512,256]{1,0:T(8,128)(2,1)S(1)} %collective-permute-done.8.refs_4_), channel_id=1, source_target_pairs={{0,2},{1,3},{2,6},{3,7},{4,0},{5,1},{6,4},{7,5},{8,10},{9,11},{10,... | collective-permute-start | bytes 786440 | tf_op jit(solution)/shard_map/ppermute | solution.py:352
  48.9 10.1 %collective-permute-start.11 = (bf16[512,256]{1,0:T(8,128)(2,1)S(1)}, bf16[512,256]{1,0:T(8,128)(2,1)S(1)}, u32[]{:S(2)}, u32[]{:S(2)}) collective-permute-start(bf16[512,256]{1,0:T(8,128)(2,1)S(1)} %collective-permute-done.7.refs_4_), channel_id=1, source_target_pairs={{0,2},{1,3},{2,6},{3,7},{4,0},{5,1},{6,4},{7,5},{8,10},{9,11},{10,... | collective-permute-start | bytes 786440 | tf_op jit(solution)/shard_map/ppermute | solution.py:352
  66.9 10.1 %collective-permute-start.18 = (bf16[64,2048]{1,0:T(8,128)(2,1)S(1)}, bf16[64,2048]{1,0:T(8,128)(2,1)S(1)}, u32[]{:S(2)}, u32[]{:S(2)}) collective-permute-start(bf16[64,2048]{1,0:T(8,128)(2,1)S(1)} %get-tuple-element.134), channel_id=1, source_target_pairs={{0,2},{1,3},{2,6},{3,7},{4,0},{5,1},{6,4},{7,5},{8,10},{9,11},{10,... | collective-permute-start | bytes 786440 | tf_op jit(solution)/shard_map/ppermute | solution.py:352
  72.3 10.3 %collective-permute-start.17 = (bf16[64,2048]{1,0:T(8,128)(2,1)S(1)}, bf16[64,2048]{1,0:T(8,128)(2,1)S(1)}, u32[]{:S(2)}, u32[]{:S(2)}) collective-permute-start(bf16[64,2048]{1,0:T(8,128)(2,1)S(1)} %get-tuple-element.137), channel_id=1, source_target_pairs={{0,2},{1,3},{2,6},{3,7},{4,0},{5,1},{6,4},{7,5},{8,10},{9,11},{10,... | collective-permute-start | bytes 786440 | tf_op jit(solution)/shard_map/ppermute | solution.py:352
  76.9 13.9 %collective-permute-start.20 = (bf16[64,2048]{1,0:T(8,128)(2,1)S(1)}, bf16[64,2048]{1,0:T(8,128)(2,1)S(1)}, u32[]{:S(2)}, u32[]{:S(2)}) collective-permute-start(bf16[64,2048]{1,0:T(8,128)(2,1)S(1)} %collective-permute-done.18.rows_ref), channel_id=1, source_target_pairs={{0,2},{1,3},{2,6},{3,7},{4,0},{5,1},{6,4},{7,5},{8,10},{9,11},{10,... | collective-permute-start | bytes 786440 | tf_op jit(solution)/shard_map/ppermute | solution.py:352
  82.5 12.9 %collective-permute-start.19 = (bf16[64,2048]{1,0:T(8,128)(2,1)S(1)}, bf16[64,2048]{1,0:T(8,128)(2,1)S(1)}, u32[]{:S(2)}, u32[]{:S(2)}) collective-permute-start(bf16[64,2048]{1,0:T(8,128)(2,1)S(1)} %collective-permute-done.17.rows_ref), channel_id=1, source_target_pairs={{0,2},{1,3},{2,6},{3,7},{4,0},{5,1},{6,4},{7,5},{8,10},{9,11},{10,... | collective-permute-start | bytes 786440 | tf_op jit(solution)/shard_map/ppermute | solution.py:352
  85.0 16.7 %collective-permute-start.23 = (bf16[64,2048]{1,0:T(8,128)(2,1)S(1)}, bf16[64,2048]{1,0:T(8,128)(2,1)S(1)}, u32[]{:S(2)}, u32[]{:S(2)}) collective-permute-start(bf16[64,2048]{1,0:T(8,128)(2,1)S(1)} %convert_element_type.36), channel_id=1, source_target_pairs={{0,2},{1,3},{2,6},{3,7},{4,0},{5,1},{6,4},{7,5},{8,10},{9,11},{10,... | collective-permute-start | bytes 786440 | tf_op jit(solution)/shard_map/ppermute | solution.py:352
  90.7 14.3 %collective-permute-start.26 = (bf16[64,2048]{1,0:T(8,128)(2,1)S(1)}, bf16[64,2048]{1,0:T(8,128)(2,1)S(1)}, u32[]{:S(2)}, u32[]{:S(2)}) collective-permute-start(bf16[64,2048]{1,0:T(8,128)(2,1)S(1)} %convert_element_type.41), channel_id=1, source_target_pairs={{0,2},{1,3},{2,6},{3,7},{4,0},{5,1},{6,4},{7,5},{8,10},{9,11},{10,... | collective-permute-start | bytes 786440 | tf_op jit(solution)/shard_map/ppermute | solution.py:352
  90.8 19.8 %collective-permute-start.22 = (bf16[64,2048]{1,0:T(8,128)(2,1)S(1)}, bf16[64,2048]{1,0:T(8,128)(2,1)S(1)}, u32[]{:S(2)}, u32[]{:S(2)}) collective-permute-start(bf16[64,2048]{1,0:T(8,128)(2,1)S(1)} %collective-permute-done.20.rows_ref), channel_id=1, source_target_pairs={{0,2},{1,3},{2,6},{3,7},{4,0},{5,1},{6,4},{7,5},{8,10},{9,11},{10,... | collective-permute-start | bytes 786440 | tf_op jit(solution)/shard_map/ppermute | solution.py:352
  95.4 20.8 %collective-permute-start.21 = (bf16[64,2048]{1,0:T(8,128)(2,1)S(1)}, bf16[64,2048]{1,0:T(8,128)(2,1)S(1)}, u32[]{:S(2)}, u32[]{:S(2)}) collective-permute-start(bf16[64,2048]{1,0:T(8,128)(2,1)S(1)} %collective-permute-done.19.rows_ref), channel_id=1, source_target_pairs={{0,2},{1,3},{2,6},{3,7},{4,0},{5,1},{6,4},{7,5},{8,10},{9,11},{10,... | collective-permute-start | bytes 786440 | tf_op jit(solution)/shard_map/ppermute | solution.py:352
  101.8 20.1 %collective-permute-start.24 = (bf16[64,2048]{1,0:T(8,128)(2,1)S(1)}, bf16[64,2048]{1,0:T(8,128)(2,1)S(1)}, u32[]{:S(2)}, u32[]{:S(2)}) collective-permute-start(bf16[64,2048]{1,0:T(8,128)(2,1)S(1)} %add_convert_fusion.3), channel_id=1, source_target_pairs={{0,2},{1,3},{2,6},{3,7},{4,0},{5,1},{6,4},{7,5},{8,10},{9,11},{10,... | collective-permute-start | bytes 786440 | tf_op jit(solution)/shard_map/ppermute | solution.py:352
  105.1 22.4 %collective-permute-start.27 = (bf16[64,2048]{1,0:T(8,128)(2,1)S(1)}, bf16[64,2048]{1,0:T(8,128)(2,1)S(1)}, u32[]{:S(2)}, u32[]{:S(2)}) collective-permute-start(bf16[64,2048]{1,0:T(8,128)(2,1)S(1)} %add_convert_fusion.1), channel_id=1, source_target_pairs={{0,2},{1,3},{2,6},{3,7},{4,0},{5,1},{6,4},{7,5},{8,10},{9,11},{10,... | collective-permute-start | bytes 786440 | tf_op jit(solution)/shard_map/ppermute | solution.py:352
  121.9 13.7 %collective-permute-start.25 = (bf16[64,2048]{1,0:T(8,128)(2,1)S(1)}, bf16[64,2048]{1,0:T(8,128)(2,1)S(1)}, u32[]{:S(2)}, u32[]{:S(2)}) collective-permute-start(bf16[64,2048]{1,0:T(8,128)(2,1)S(1)} %add_convert_fusion.2), channel_id=1, source_target_pairs={{0,2},{1,3},{2,6},{3,7},{4,0},{5,1},{6,4},{7,5},{8,10},{9,11},{10,... | collective-permute-start | bytes 786440 | tf_op jit(solution)/shard_map/ppermute | solution.py:352
  127.5 10.8 %collective-permute-start.28 = (bf16[64,2048]{1,0:T(8,128)(2,1)S(1)}, bf16[64,2048]{1,0:T(8,128)(2,1)S(1)}, u32[]{:S(2)}, u32[]{:S(2)}) collective-permute-start(bf16[64,2048]{1,0:T(8,128)(2,1)S(1)} %add_convert_fusion), channel_id=1, source_target_pairs={{0,2},{1,3},{2,6},{3,7},{4,0},{5,1},{6,4},{7,5},{8,10},{9,11},{10,... | collective-permute-start | bytes 786440 | tf_op jit(solution)/shard_map/ppermute | solution.py:352
  (16 other events, 122.1 us)

commit v4 on v3

--- a/solution.py
+++ b/solution.py
@@ -62,6 +62,9 @@
     parts = [jnp.concatenate([ref[...] for ref in block_refs], axis=0)]
     if first:
         parts.insert(0, own_ref[...])
+    summing = [
+        jnp.concatenate([part[:, head_size:], jnp.ones_like(part[:, head_size:])], axis=1) for part in parts
+    ]
 
     def stacked(ref, start):
         return jnp.concatenate(
@@ -96,12 +99,12 @@
             denominator = (
                 jnp.concatenate([denominator_in[start + h] for h in range(group)], axis=0) * rescale
             )
-        for part, ref in zip(scores, parts):
+        for part, keyed in zip(scores, summing):
             exponent = jnp.exp2(part - highest)
-            total = jnp.sum(exponent, axis=-1, keepdims=True)
             product = jnp.dot(
-                exponent.astype(jnp.bfloat16), ref[:, head_size:], preferred_element_type=jnp.float32
+                exponent.astype(jnp.bfloat16), keyed, preferred_element_type=jnp.float32
             )
+            product, total = product[:, :head_size], product[:, head_size : head_size + 1]
             weighted = product if weighted is None else weighted + product
             denominator = total if denominator is None else denominator + total
         if last:

time: 140 us -> 139 us (level)
  waiting for transfers between devices: 24.4 us -> 27 us
  Pallas kernels: 71 us -> 68.6 us
    ppermute x18, waiting for transfers between devices: 22 us -> 24.6 us  [shards(): ring = lambda block: lax.ppermute(block, 'member', ring_pairs)]
    pallas_call x9, Pallas kernels: 30.2 us -> 27.9 us  [attend(): pl.pallas_call(functools.partial(attend_kernel, first, last, head_size, m...]
  transfers between devices with their start and end apart: 29 -> 29, of which waited for: 12 -> 12; matrix products, arithmetic and copies ran while one was open for 3% -> 3% of each run, Pallas kernels for 48% -> 47%
where the time goes in v4:
time: 139 us
  Pallas kernels  68.6 us (49%)
  starting transfers between devices  35.4 us (25%)
  waiting for transfers between devices  27 us (19%)
  other arithmetic  5.4 us (4%)
  between operations  2.23 us (2%)
    ppermute x18, starting transfers between devices, shards(): ring = lambda block: lax.ppermute(block, 'member', ring_pairs)  30 us
    pallas_call x9, Pallas kernels, attend(): pl.pallas_call(functools.partial(attend_kernel, first, last, head_size, m...  27.9 us
    pallas_call x7, Pallas kernels, feed_forward(): pl.pallas_call(functools.partial(feed_forward_kernel, len(expands)), in_s...  26.7 us
    ppermute x18, waiting for transfers between devices, shards(): ring = lambda block: lax.ppermute(block, 'member', ring_pairs)  24.6 us
    pallas_call x1, Pallas kernels, project(): pl.pallas_call(functools.partial(project_kernel, factor), in_specs=[insid...  6.27 us
    ppermute x2, starting transfers between devices, step(): return lax.ppermute(block, ('group', 'member'), pairs)  4.52 us
    pallas_call x1, Pallas kernels, hold(): pl.pallas_call(functools.partial(hold_kernel, count), in_specs=[pl.BlockS...  4.12 us
    pallas_call x2, Pallas kernels, finish(): pl.pallas_call(functools.partial(finish_kernel, share), in_specs=[inside]...  3.63 us
  transfers between devices with their start and end apart: 29, of which 12 were waited for; matrix products, arithmetic and copies ran while one was open for 3% of the time, Pallas kernels for 47%

profile of v4, /device:TPU:0, one launch (start us, length us, event | category | flops | bytes accessed | tf_op | source)
XLA Modules:
  0.0 138.7 jit_solution(9295573055573917704)
XLA Ops:
  0.5 2.9 %collective-permute-start = (bf16[1024,256]{1,0:T(8,128)(2,1)}, bf16[1024,256]{1,0:T(8,128)(2,1)S(1)}, u32[]{:S(2)}, u32[]{:S(2)}) collective-permute-start(bf16[1024,256]{1,0:T(8,128)(2,1)} %bitcast.23), channel_id=1, source_target_pairs={{0,8},{1,17},{2,10},{3,19},{4,12},{5,21},{6,14},{7,23},{8,0},{9,25... | collective-permute-start | bytes 1572872 | tf_op jit(solution)/shard_map/ppermute | solution.py:269
  5.4 6.3 %shard_map.136 = (bf16[128,2048]{1,0:T(8,128)(2,1)}, bf16[128,256]{1,0:T(8,128)(2,1)}) custom-call(bf16[128,2048]{1,0:T(8,128)(2,1)} %bitcast.16, f32[1,2048]{1,0:T(1,128)} %bitcast.24, f32[1,2048]{1,0:T(1,128)} %bitcast.25, bf16[2048,2048]{1,0:T(8,128)(2,1)} %query_ref.1, bf16[2048,256]{1,0:T(8,128)(2,1)} %keyval_ref.1), custom_call_target="tpu_custom_call" | custom-call | flops 1207959552 | bytes 9437184 | tf_op jit(solution)/shard_map/pallas_call | solution.py:311
  14.5 4.1 %shard_map.137 = (bf16[2048,1024]{1,0:T(8,128)(2,1)S(1)}, bf16[1024,2048]{1,0:T(8,128)(2,1)S(1)}, f32[8,128]{1,0:T(8,128)}) custom-call(bf16[2048,1024]{1,0:T(8,128)(2,1)} %refs_0_.1, bf16[1024,2048]{1,0:T(8,128)(2,1)} %refs_1_.1), custom_call_target="tpu_custom_call" | custom-call | bytes 8388608 | tf_op jit(solution)/shard_map/pallas_call | solution.py:189
  22.9 2.6 %collective-permute-start.4 = (bf16[512,256]{1,0:T(8,128)(2,1)S(1)}, bf16[512,256]{1,0:T(8,128)(2,1)S(1)}, u32[]{:S(2)}, u32[]{:S(2)}) collective-permute-start(bf16[512,256]{1,0:T(8,128)(2,1)S(1)} %get-tuple-element.156.refs_3_), channel_id=1, source_target_pairs={{0,2},{1,3},{2,6},{3,7},{4,0},{5,1},{6,4},{7,5},{8,10},{9,11},{10,... | collective-permute-start | bytes 786440 | tf_op jit(solution)/shard_map/ppermute | solution.py:355
  25.5 3.5 %shard_map.138 = (f32[128,2048]{1,0:T(8,128)S(1)}, f32[16,128,1]{2,1,0:T(8,128)S(1)}, f32[16,128,1]{2,1,0:T(8,128)S(1)}, bf16[2048,1024]{1,0:T(8,128)(2,1)S(1)}) custom-call(bf16[128,2048]{1,0:T(8,128)(2,1)S(1)} %copy-done, bf16[128,256]{1,0:T(8,128)(2,1)S(1)} %copy-done.3, bf16[512,256]{1,0:T(8,128)(2,1)S(1)} %get-tuple-element.155.refs_2_, ...), custom_call_target="tpu_custom_call" | custom-call | flops 1207959552 | bytes 2686976 | tf_op jit(solution)/shard_map/pallas_call | solution.py:155
  32.1 3.5 %shard_map.139 = (f32[128,2048]{1,0:T(8,128)S(1)}, f32[16,128,1]{2,1,0:T(8,128)S(1)}, f32[16,128,1]{2,1,0:T(8,128)S(1)}, bf16[1024,2048]{1,0:T(8,128)(2,1)S(1)}) custom-call(bf16[128,2048]{1,0:T(8,128)(2,1)S(1)} %copy-done, f32[128,2048]{1,0:T(8,128)S(1)} %get-tuple-element.90.refs_1_, f32[16,128,1]{2,1,0:T(8,128)S(1)} %get-tuple-element.91.refs_2_, ...), custom_call_target="tpu_custom_call" | custom-call | flops 1073741824 | bytes 2621440 | tf_op jit(solution)/shard_map/pallas_call | solution.py:155
  39.3 3.5 %shard_map.140 = (f32[128,2048]{1,0:T(8,128)S(1)}, f32[16,128,1]{2,1,0:T(8,128)S(1)}, f32[16,128,1]{2,1,0:T(8,128)S(1)}) custom-call(bf16[128,2048]{1,0:T(8,128)(2,1)S(1)} %copy-done, f32[128,2048]{1,0:T(8,128)S(1)} %get-tuple-element.99.refs_1_, f32[16,128,1]{2,1,0:T(8,128)S(1)} %get-tuple-element.100.refs_2_, ...), custom_call_target="tpu_custom_call" | custom-call | flops 1073741824 | bytes 2621440 | tf_op jit(solution)/shard_map/pallas_call | solution.py:155
  44.9 3.5 %shard_map.141 = (f32[128,2048]{1,0:T(8,128)S(1)}, f32[16,128,1]{2,1,0:T(8,128)S(1)}, f32[16,128,1]{2,1,0:T(8,128)S(1)}) custom-call(bf16[128,2048]{1,0:T(8,128)(2,1)S(1)} %copy-done, f32[128,2048]{1,0:T(8,128)S(1)} %get-tuple-element.105.refs_1_, f32[16,128,1]{2,1,0:T(8,128)S(1)} %get-tuple-element.106.refs_2_, ...), custom_call_target="tpu_custom_call" | custom-call | flops 1073741824 | bytes 2621440 | tf_op jit(solution)/shard_map/pallas_call | solution.py:155
  50.5 3.5 %shard_map.142 = (f32[128,2048]{1,0:T(8,128)S(1)}, f32[16,128,1]{2,1,0:T(8,128)S(1)}, f32[16,128,1]{2,1,0:T(8,128)S(1)}) custom-call(bf16[128,2048]{1,0:T(8,128)(2,1)S(1)} %copy-done, f32[128,2048]{1,0:T(8,128)S(1)} %get-tuple-element.113.refs_1_, f32[16,128,1]{2,1,0:T(8,128)S(1)} %get-tuple-element.114.refs_2_, ...), custom_call_target="tpu_custom_call" | custom-call | flops 1073741824 | bytes 2621440 | tf_op jit(solution)/shard_map/pallas_call | solution.py:155
  54.1 3.5 %shard_map.143 = (f32[128,2048]{1,0:T(8,128)S(1)}, f32[16,128,1]{2,1,0:T(8,128)S(1)}, f32[16,128,1]{2,1,0:T(8,128)S(1)}) custom-call(bf16[128,2048]{1,0:T(8,128)(2,1)S(1)} %copy-done, f32[128,2048]{1,0:T(8,128)S(1)} %get-tuple-element.119.refs_1_, f32[16,128,1]{2,1,0:T(8,128)S(1)} %get-tuple-element.120.refs_2_, ...), custom_call_target="tpu_custom_call" | custom-call | flops 1073741824 | bytes 2621440 | tf_op jit(solution)/shard_map/pallas_call | solution.py:155
  59.1 3.5 %shard_map.144 = (f32[128,2048]{1,0:T(8,128)S(1)}, f32[16,128,1]{2,1,0:T(8,128)S(1)}, f32[16,128,1]{2,1,0:T(8,128)S(1)}) custom-call(bf16[128,2048]{1,0:T(8,128)(2,1)S(1)} %copy-done, f32[128,2048]{1,0:T(8,128)S(1)} %get-tuple-element.126.refs_1_, f32[16,128,1]{2,1,0:T(8,128)S(1)} %get-tuple-element.127.refs_2_, ...), custom_call_target="tpu_custom_call" | custom-call | flops 1073741824 | bytes 2621440 | tf_op jit(solution)/shard_map/pallas_call | solution.py:155
  70.8 3.3 %collective-permute-start.17 = (bf16[64,2048]{1,0:T(8,128)(2,1)S(1)}, bf16[64,2048]{1,0:T(8,128)(2,1)S(1)}, u32[]{:S(2)}, u32[]{:S(2)}) collective-permute-start(bf16[64,2048]{1,0:T(8,128)(2,1)S(1)} %get-tuple-element.137), channel_id=1, source_target_pairs={{0,2},{1,3},{2,6},{3,7},{4,0},{5,1},{6,4},{7,5},{8,10},{9,11},{10,... | collective-permute-start | bytes 786440 | tf_op jit(solution)/shard_map/ppermute | solution.py:355
  77.1 3.8 %shard_map.149 = f32[64,2048]{1,0:T(8,128)S(1)} custom-call(bf16[64,2048]{1,0:T(8,128)(2,1)S(1)} %collective-permute-done.18.rows_ref, bf16[2048,1024]{1,0:T(8,128)(2,1)S(1)} %get-tuple-element.138.refs_0_, bf16[2048,1024]{1,0:T(8,128)(2,1)S(1)} %get-tuple-element.139.refs_1_, bf16[1024,2048]{1,0:T(8,128)(2,1)S(1)} %get-tuple-element.140.refs_2_, ...), custom_call_target="tpu_custom_call" | custom-call | tf_op jit(solution)/shard_map/pallas_call | solution.py:216
  81.9 2.4 %collective-permute-start.19 = (bf16[64,2048]{1,0:T(8,128)(2,1)S(1)}, bf16[64,2048]{1,0:T(8,128)(2,1)S(1)}, u32[]{:S(2)}, u32[]{:S(2)}) collective-permute-start(bf16[64,2048]{1,0:T(8,128)(2,1)S(1)} %collective-permute-done.17.rows_ref), channel_id=1, source_target_pairs={{0,2},{1,3},{2,6},{3,7},{4,0},{5,1},{6,4},{7,5},{8,10},{9,11},{10,... | collective-permute-start | bytes 786440 | tf_op jit(solution)/shard_map/ppermute | solution.py:355
  86.2 3.8 %shard_map.150 = f32[64,2048]{1,0:T(8,128)S(1)} custom-call(bf16[64,2048]{1,0:T(8,128)(2,1)S(1)} %collective-permute-done.17.rows_ref, bf16[2048,1024]{1,0:T(8,128)(2,1)S(1)} %get-tuple-element.138.refs_0_, bf16[2048,1024]{1,0:T(8,128)(2,1)S(1)} %get-tuple-element.139.refs_1_, bf16[1024,2048]{1,0:T(8,128)(2,1)S(1)} %get-tuple-element.140.refs_2_, ...), custom_call_target="tpu_custom_call" | custom-call | tf_op jit(solution)/shard_map/pallas_call | solution.py:216
  90.9 3.8 %shard_map.151 = f32[64,2048]{1,0:T(8,128)S(1)} custom-call(bf16[64,2048]{1,0:T(8,128)(2,1)S(1)} %collective-permute-done.20.rows_ref, bf16[2048,1024]{1,0:T(8,128)(2,1)S(1)} %get-tuple-element.138.refs_0_, bf16[2048,1024]{1,0:T(8,128)(2,1)S(1)} %get-tuple-element.139.refs_1_, bf16[1024,2048]{1,0:T(8,128)(2,1)S(1)} %get-tuple-element.140.refs_2_, ...), custom_call_target="tpu_custom_call" | custom-call | tf_op jit(solution)/shard_map/pallas_call | solution.py:216
  94.8 2.5 %collective-permute-start.21 = (bf16[64,2048]{1,0:T(8,128)(2,1)S(1)}, bf16[64,2048]{1,0:T(8,128)(2,1)S(1)}, u32[]{:S(2)}, u32[]{:S(2)}) collective-permute-start(bf16[64,2048]{1,0:T(8,128)(2,1)S(1)} %collective-permute-done.19.rows_ref), channel_id=1, source_target_pairs={{0,2},{1,3},{2,6},{3,7},{4,0},{5,1},{6,4},{7,5},{8,10},{9,11},{10,... | collective-permute-start | bytes 786440 | tf_op jit(solution)/shard_map/ppermute | solution.py:355
  97.3 3.8 %shard_map.152 = f32[64,2048]{1,0:T(8,128)S(1)} custom-call(bf16[64,2048]{1,0:T(8,128)(2,1)S(1)} %collective-permute-done.19.rows_ref, bf16[2048,1024]{1,0:T(8,128)(2,1)S(1)} %get-tuple-element.138.refs_0_, bf16[2048,1024]{1,0:T(8,128)(2,1)S(1)} %get-tuple-element.139.refs_1_, bf16[1024,2048]{1,0:T(8,128)(2,1)S(1)} %get-tuple-element.140.refs_2_, ...), custom_call_target="tpu_custom_call" | custom-call | tf_op jit(solution)/shard_map/pallas_call | solution.py:216
  105.9 4.2 %collective-permute-done.22.rows_ref = bf16[64,2048]{1,0:T(8,128)(2,1)S(1)} collective-permute-done((bf16[64,2048]{1,0:T(8,128)(2,1)S(1)}, bf16[64,2048]{1,0:T(8,128)(2,1)S(1)}, u32[]{:S(2)}, u32[]{:S(2)}) %collective-permute-start.22) | collective-permute-done | bytes 262176 | tf_op jit(solution)/shard_map/ppermute | solution.py:355
  110.0 3.8 %shard_map.153 = f32[64,2048]{1,0:T(8,128)S(1)} custom-call(bf16[64,2048]{1,0:T(8,128)(2,1)S(1)} %collective-permute-done.22.rows_ref, bf16[2048,1024]{1,0:T(8,128)(2,1)S(1)} %get-tuple-element.138.refs_0_, bf16[2048,1024]{1,0:T(8,128)(2,1)S(1)} %get-tuple-element.139.refs_1_, bf16[1024,2048]{1,0:T(8,128)(2,1)S(1)} %get-tuple-element.140.refs_2_, ...), custom_call_target="tpu_custom_call" | custom-call | tf_op jit(solution)/shard_map/pallas_call | solution.py:216
  115.6 3.8 %shard_map.154 = f32[64,2048]{1,0:T(8,128)S(1)} custom-call(bf16[64,2048]{1,0:T(8,128)(2,1)S(1)} %collective-permute-done.21.rows_ref, bf16[2048,1024]{1,0:T(8,128)(2,1)S(1)} %get-tuple-element.138.refs_0_, bf16[2048,1024]{1,0:T(8,128)(2,1)S(1)} %get-tuple-element.139.refs_1_, bf16[1024,2048]{1,0:T(8,128)(2,1)S(1)} %get-tuple-element.140.refs_2_, ...), custom_call_target="tpu_custom_call" | custom-call | tf_op jit(solution)/shard_map/pallas_call | solution.py:216
  122.7 4.2 %collective-permute-done.27 = bf16[64,2048]{1,0:T(8,128)(2,1)S(1)} collective-permute-done((bf16[64,2048]{1,0:T(8,128)(2,1)S(1)}, bf16[64,2048]{1,0:T(8,128)(2,1)S(1)}, u32[]{:S(2)}, u32[]{:S(2)}) %collective-permute-start.27) | collective-permute-done | bytes 262176 | tf_op jit(solution)/shard_map/ppermute | solution.py:355
  129.0 3.7 %shard_map.155 = f32[128,2048]{1,0:T(8,128)S(1)} custom-call(bf16[128,2048]{1,0:T(8,128)(2,1)S(1)} %pad_maximum_fusion.rows_ref, bf16[2048,1024]{1,0:T(8,128)(2,1)S(1)} %get-tuple-element.138.refs_0_, bf16[2048,1024]{1,0:T(8,128)(2,1)S(1)} %get-tuple-element.139.refs_1_, bf16[1024,2048]{1,0:T(8,128)(2,1)S(1)} %get-tuple-element.140.refs_2_, ...), custom_call_target="tpu_custom_call" | custom-call | tf_op jit(solution)/shard_map/pallas_call | solution.py:216
  134.7 3.0 %collective-permute-done.28 = bf16[64,2048]{1,0:T(8,128)(2,1)S(1)} collective-permute-done((bf16[64,2048]{1,0:T(8,128)(2,1)S(1)}, bf16[64,2048]{1,0:T(8,128)(2,1)S(1)}, u32[]{:S(2)}, u32[]{:S(2)}) %collective-permute-start.28) | collective-permute-done | bytes 262176 | tf_op jit(solution)/shard_map/ppermute | solution.py:355
  (92 shorter events, 49.9 us)
Async XLA Ops:
  0.0 11.7 %collective-permute-start.1 = (bf16[2048,1024]{1,0:T(8,128)(2,1)}, bf16[2048,1024]{1,0:T(8,128)(2,1)}, u32[]{:S(2)}, u32[]{:S(2)}) collective-permute-start(bf16[2048,1024]{1,0:T(8,128)(2,1)} %refs_0_.1), channel_id=1, source_target_pairs={{0,1},{1,0},{2,3},{3,2},{4,5},{5,4},{6,7},{7,6},{8,9},{9,8},{10,11... | collective-permute-start | bytes 12582920 | tf_op jit(solution)/shard_map/ppermute | solution.py:356
  0.5 20.7 %collective-permute-start.3 = (bf16[1024,2048]{1,0:T(8,128)(2,1)}, bf16[1024,2048]{1,0:T(8,128)(2,1)}, u32[]{:S(2)}, u32[]{:S(2)}) collective-permute-start(bf16[1024,2048]{1,0:T(8,128)(2,1)} %refs_1_.1), channel_id=1, source_target_pairs={{0,1},{1,0},{2,3},{3,2},{4,5},{5,4},{6,7},{7,6},{8,9},{9,8},{10,11... | collective-permute-start | bytes 12582920 | tf_op jit(solution)/shard_map/ppermute | solution.py:356
  0.5 11.2 %collective-permute-start = (bf16[1024,256]{1,0:T(8,128)(2,1)}, bf16[1024,256]{1,0:T(8,128)(2,1)S(1)}, u32[]{:S(2)}, u32[]{:S(2)}) collective-permute-start(bf16[1024,256]{1,0:T(8,128)(2,1)} %bitcast.23), channel_id=1, source_target_pairs={{0,8},{1,17},{2,10},{3,19},{4,12},{5,21},{6,14},{7,23},{8,0},{9,25... | collective-permute-start | bytes 1572872 | tf_op jit(solution)/shard_map/ppermute | solution.py:269
  11.8 9.2 %collective-permute-start.2 = (bf16[1024,256]{1,0:T(8,128)(2,1)S(1)}, bf16[1024,256]{1,0:T(8,128)(2,1)S(1)}, u32[]{:S(2)}, u32[]{:S(2)}) collective-permute-start(bf16[1024,256]{1,0:T(8,128)(2,1)S(1)} %broadcast_select_fusion), channel_id=1, source_target_pairs={{0,16},{1,9},{2,18},{3,11},{4,20},{5,13},{6,22},{7,15},{8,24},{9,1... | collective-permute-start | bytes 1572872 | tf_op jit(solution)/shard_map/ppermute | solution.py:269
  21.1 11.0 %collective-permute-start.6 = (bf16[1024,256]{1,0:T(8,128)(2,1)S(1)}, bf16[1024,256]{1,0:T(8,128)(2,1)S(1)}, u32[]{:S(2)}, u32[]{:S(2)}) collective-permute-start(bf16[1024,256]{1,0:T(8,128)(2,1)S(1)} %select_select_fusion), channel_id=1, source_target_pairs={{0,1},{1,0},{2,3},{3,2},{4,5},{5,4},{6,7},{7,6},{8,9},{9,8},{10,11... | collective-permute-start | bytes 1572872 | tf_op jit(solution)/shard_map/ppermute | solution.py:356
  21.2 10.1 %collective-permute-start.5 = (bf16[512,256]{1,0:T(8,128)(2,1)S(1)}, bf16[512,256]{1,0:T(8,128)(2,1)S(1)}, u32[]{:S(2)}, u32[]{:S(2)}) collective-permute-start(bf16[512,256]{1,0:T(8,128)(2,1)S(1)} %get-tuple-element.155.refs_2_), channel_id=1, source_target_pairs={{0,2},{1,3},{2,6},{3,7},{4,0},{5,1},{6,4},{7,5},{8,10},{9,11},{10,... | collective-permute-start | bytes 786440 | tf_op jit(solution)/shard_map/ppermute | solution.py:355
  22.9 14.0 %collective-permute-start.4 = (bf16[512,256]{1,0:T(8,128)(2,1)S(1)}, bf16[512,256]{1,0:T(8,128)(2,1)S(1)}, u32[]{:S(2)}, u32[]{:S(2)}) collective-permute-start(bf16[512,256]{1,0:T(8,128)(2,1)S(1)} %get-tuple-element.156.refs_3_), channel_id=1, source_target_pairs={{0,2},{1,3},{2,6},{3,7},{4,0},{5,1},{6,4},{7,5},{8,10},{9,11},{10,... | collective-permute-start | bytes 786440 | tf_op jit(solution)/shard_map/ppermute | solution.py:355
  31.3 8.0 %collective-permute-start.9 = (bf16[512,256]{1,0:T(8,128)(2,1)S(1)}, bf16[512,256]{1,0:T(8,128)(2,1)S(1)}, u32[]{:S(2)}, u32[]{:S(2)}) collective-permute-start(bf16[512,256]{1,0:T(8,128)(2,1)S(1)} %collective-permute-done.5.refs_4_), channel_id=1, source_target_pairs={{0,1},{1,0},{2,3},{3,2},{4,5},{5,4},{6,7},{7,6},{8,9},{9,8},{10,11... | collective-permute-start | bytes 786440 | tf_op jit(solution)/shard_map/ppermute | solution.py:356
  31.3 11.5 %collective-permute-start.8 = (bf16[512,256]{1,0:T(8,128)(2,1)S(1)}, bf16[512,256]{1,0:T(8,128)(2,1)S(1)}, u32[]{:S(2)}, u32[]{:S(2)}) collective-permute-start(bf16[512,256]{1,0:T(8,128)(2,1)S(1)} %collective-permute-done.5.refs_4_), channel_id=1, source_target_pairs={{0,2},{1,3},{2,6},{3,7},{4,0},{5,1},{6,4},{7,5},{8,10},{9,11},{10,... | collective-permute-start | bytes 786440 | tf_op jit(solution)/shard_map/ppermute | solution.py:355
  36.9 11.4 %collective-permute-start.7 = (bf16[512,256]{1,0:T(8,128)(2,1)S(1)}, bf16[512,256]{1,0:T(8,128)(2,1)S(1)}, u32[]{:S(2)}, u32[]{:S(2)}) collective-permute-start(bf16[512,256]{1,0:T(8,128)(2,1)S(1)} %collective-permute-done.4.refs_4_), channel_id=1, source_target_pairs={{0,2},{1,3},{2,6},{3,7},{4,0},{5,1},{6,4},{7,5},{8,10},{9,11},{10,... | collective-permute-start | bytes 786440 | tf_op jit(solution)/shard_map/ppermute | solution.py:355
  42.9 11.1 %collective-permute-start.12 = (bf16[512,256]{1,0:T(8,128)(2,1)S(1)}, bf16[512,256]{1,0:T(8,128)(2,1)S(1)}, u32[]{:S(2)}, u32[]{:S(2)}) collective-permute-start(bf16[512,256]{1,0:T(8,128)(2,1)S(1)} %collective-permute-done.8.refs_4_), channel_id=1, source_target_pairs={{0,2},{1,3},{2,6},{3,7},{4,0},{5,1},{6,4},{7,5},{8,10},{9,11},{10,... | collective-permute-start | bytes 786440 | tf_op jit(solution)/shard_map/ppermute | solution.py:355
  48.4 10.6 %collective-permute-start.11 = (bf16[512,256]{1,0:T(8,128)(2,1)S(1)}, bf16[512,256]{1,0:T(8,128)(2,1)S(1)}, u32[]{:S(2)}, u32[]{:S(2)}) collective-permute-start(bf16[512,256]{1,0:T(8,128)(2,1)S(1)} %collective-permute-done.7.refs_4_), channel_id=1, source_target_pairs={{0,2},{1,3},{2,6},{3,7},{4,0},{5,1},{6,4},{7,5},{8,10},{9,11},{10,... | collective-permute-start | bytes 786440 | tf_op jit(solution)/shard_map/ppermute | solution.py:355
  66.2 10.1 %collective-permute-start.18 = (bf16[64,2048]{1,0:T(8,128)(2,1)S(1)}, bf16[64,2048]{1,0:T(8,128)(2,1)S(1)}, u32[]{:S(2)}, u32[]{:S(2)}) collective-permute-start(bf16[64,2048]{1,0:T(8,128)(2,1)S(1)} %get-tuple-element.134), channel_id=1, source_target_pairs={{0,2},{1,3},{2,6},{3,7},{4,0},{5,1},{6,4},{7,5},{8,10},{9,11},{10,... | collective-permute-start | bytes 786440 | tf_op jit(solution)/shard_map/ppermute | solution.py:355
  70.8 11.1 %collective-permute-start.17 = (bf16[64,2048]{1,0:T(8,128)(2,1)S(1)}, bf16[64,2048]{1,0:T(8,128)(2,1)S(1)}, u32[]{:S(2)}, u32[]{:S(2)}) collective-permute-start(bf16[64,2048]{1,0:T(8,128)(2,1)S(1)} %get-tuple-element.137), channel_id=1, source_target_pairs={{0,2},{1,3},{2,6},{3,7},{4,0},{5,1},{6,4},{7,5},{8,10},{9,11},{10,... | collective-permute-start | bytes 786440 | tf_op jit(solution)/shard_map/ppermute | solution.py:355
  76.3 13.9 %collective-permute-start.20 = (bf16[64,2048]{1,0:T(8,128)(2,1)S(1)}, bf16[64,2048]{1,0:T(8,128)(2,1)S(1)}, u32[]{:S(2)}, u32[]{:S(2)}) collective-permute-start(bf16[64,2048]{1,0:T(8,128)(2,1)S(1)} %collective-permute-done.18.rows_ref), channel_id=1, source_target_pairs={{0,2},{1,3},{2,6},{3,7},{4,0},{5,1},{6,4},{7,5},{8,10},{9,11},{10,... | collective-permute-start | bytes 786440 | tf_op jit(solution)/shard_map/ppermute | solution.py:355
  81.9 12.9 %collective-permute-start.19 = (bf16[64,2048]{1,0:T(8,128)(2,1)S(1)}, bf16[64,2048]{1,0:T(8,128)(2,1)S(1)}, u32[]{:S(2)}, u32[]{:S(2)}) collective-permute-start(bf16[64,2048]{1,0:T(8,128)(2,1)S(1)} %collective-permute-done.17.rows_ref), channel_id=1, source_target_pairs={{0,2},{1,3},{2,6},{3,7},{4,0},{5,1},{6,4},{7,5},{8,10},{9,11},{10,... | collective-permute-start | bytes 786440 | tf_op jit(solution)/shard_map/ppermute | solution.py:355
  84.4 16.7 %collective-permute-start.23 = (bf16[64,2048]{1,0:T(8,128)(2,1)S(1)}, bf16[64,2048]{1,0:T(8,128)(2,1)S(1)}, u32[]{:S(2)}, u32[]{:S(2)}) collective-permute-start(bf16[64,2048]{1,0:T(8,128)(2,1)S(1)} %convert_element_type.36), channel_id=1, source_target_pairs={{0,2},{1,3},{2,6},{3,7},{4,0},{5,1},{6,4},{7,5},{8,10},{9,11},{10,... | collective-permute-start | bytes 786440 | tf_op jit(solution)/shard_map/ppermute | solution.py:355
  90.1 14.3 %collective-permute-start.26 = (bf16[64,2048]{1,0:T(8,128)(2,1)S(1)}, bf16[64,2048]{1,0:T(8,128)(2,1)S(1)}, u32[]{:S(2)}, u32[]{:S(2)}) collective-permute-start(bf16[64,2048]{1,0:T(8,128)(2,1)S(1)} %convert_element_type.41), channel_id=1, source_target_pairs={{0,2},{1,3},{2,6},{3,7},{4,0},{5,1},{6,4},{7,5},{8,10},{9,11},{10,... | collective-permute-start | bytes 786440 | tf_op jit(solution)/shard_map/ppermute | solution.py:355
  90.2 19.8 %collective-permute-start.22 = (bf16[64,2048]{1,0:T(8,128)(2,1)S(1)}, bf16[64,2048]{1,0:T(8,128)(2,1)S(1)}, u32[]{:S(2)}, u32[]{:S(2)}) collective-permute-start(bf16[64,2048]{1,0:T(8,128)(2,1)S(1)} %collective-permute-done.20.rows_ref), channel_id=1, source_target_pairs={{0,2},{1,3},{2,6},{3,7},{4,0},{5,1},{6,4},{7,5},{8,10},{9,11},{10,... | collective-permute-start | bytes 786440 | tf_op jit(solution)/shard_map/ppermute | solution.py:355
  94.8 20.8 %collective-permute-start.21 = (bf16[64,2048]{1,0:T(8,128)(2,1)S(1)}, bf16[64,2048]{1,0:T(8,128)(2,1)S(1)}, u32[]{:S(2)}, u32[]{:S(2)}) collective-permute-start(bf16[64,2048]{1,0:T(8,128)(2,1)S(1)} %collective-permute-done.19.rows_ref), channel_id=1, source_target_pairs={{0,2},{1,3},{2,6},{3,7},{4,0},{5,1},{6,4},{7,5},{8,10},{9,11},{10,... | collective-permute-start | bytes 786440 | tf_op jit(solution)/shard_map/ppermute | solution.py:355
  101.2 20.1 %collective-permute-start.24 = (bf16[64,2048]{1,0:T(8,128)(2,1)S(1)}, bf16[64,2048]{1,0:T(8,128)(2,1)S(1)}, u32[]{:S(2)}, u32[]{:S(2)}) collective-permute-start(bf16[64,2048]{1,0:T(8,128)(2,1)S(1)} %add_convert_fusion.3), channel_id=1, source_target_pairs={{0,2},{1,3},{2,6},{3,7},{4,0},{5,1},{6,4},{7,5},{8,10},{9,11},{10,... | collective-permute-start | bytes 786440 | tf_op jit(solution)/shard_map/ppermute | solution.py:355
  104.5 22.4 %collective-permute-start.27 = (bf16[64,2048]{1,0:T(8,128)(2,1)S(1)}, bf16[64,2048]{1,0:T(8,128)(2,1)S(1)}, u32[]{:S(2)}, u32[]{:S(2)}) collective-permute-start(bf16[64,2048]{1,0:T(8,128)(2,1)S(1)} %add_convert_fusion.1), channel_id=1, source_target_pairs={{0,2},{1,3},{2,6},{3,7},{4,0},{5,1},{6,4},{7,5},{8,10},{9,11},{10,... | collective-permute-start | bytes 786440 | tf_op jit(solution)/shard_map/ppermute | solution.py:355
  121.3 13.3 %collective-permute-start.25 = (bf16[64,2048]{1,0:T(8,128)(2,1)S(1)}, bf16[64,2048]{1,0:T(8,128)(2,1)S(1)}, u32[]{:S(2)}, u32[]{:S(2)}) collective-permute-start(bf16[64,2048]{1,0:T(8,128)(2,1)S(1)} %add_convert_fusion.2), channel_id=1, source_target_pairs={{0,2},{1,3},{2,6},{3,7},{4,0},{5,1},{6,4},{7,5},{8,10},{9,11},{10,... | collective-permute-start | bytes 786440 | tf_op jit(solution)/shard_map/ppermute | solution.py:355
  126.9 10.8 %collective-permute-start.28 = (bf16[64,2048]{1,0:T(8,128)(2,1)S(1)}, bf16[64,2048]{1,0:T(8,128)(2,1)S(1)}, u32[]{:S(2)}, u32[]{:S(2)}) collective-permute-start(bf16[64,2048]{1,0:T(8,128)(2,1)S(1)} %add_convert_fusion), channel_id=1, source_target_pairs={{0,2},{1,3},{2,6},{3,7},{4,0},{5,1},{6,4},{7,5},{8,10},{9,11},{10,... | collective-permute-start | bytes 786440 | tf_op jit(solution)/shard_map/ppermute | solution.py:355
  (16 other events, 120.1 us)
